TPU v7x, 512 devices: a whole 4x4x16 slice. The times are simulated.
512 devices in a mesh: seq: 128 (over x_hi, z, y), head: 4 (over x_lo, core).
Axes of the slice: x: 4 (x_hi: 2, x_lo: 2; x = x_hi * 2 + x_lo), y: 4, z: 16, core: 2. Of those that a mesh axis runs over, the one named last changes fastest.
Arguments:
- layer_input: bfloat16 [16384, 2688], P('seq'), may hold values from -32 to 32
- grad_out: bfloat16 [16384, 2688], P('seq'), may hold values from -6 to 6
- doc_start: int32 [16384], P('seq'), may hold values from 0 to 16383, as said below
- w_query: bfloat16 [2688, 2048], P('seq', 'head'), may hold values from -0.125 to 0.125
- key_weight: bfloat16 [2688, 1024], P('seq', 'head'), may hold values from -0.125 to 0.125
- value_weight: bfloat16 [2688, 1024], P('seq', 'head'), may hold values from -0.125 to 0.125
- w_out: bfloat16 [2048, 2688], P('head', 'seq'), may hold values from -0.125 to 0.125
- q_gain: float32 [128], replicated, may hold values from 0.5 to 5, as said below
- key_norm_gain: float32 [128], replicated, may hold values from 0.5 to 5, as said below
Outputs:
- fisher_value: float32 [2688, 1024], P('seq', 'head')
- grad_input: bfloat16 [16384, 2688], P(('seq', 'head'))
Inputs may be any that keep to these rules, and one draw needn't show every extreme that they name: doc_start[t] is the first token of the document holding token t: it never falls, doc_start[t] <= t, doc_start[0] = 0, and the last token begins a document of its own. `q_gain`: positive. `key_norm_gain`: positive.
All inputs are finite; a program needn't handle non-finite values.
Results may differ from a plain program's by a relative error of at most 0.011.
Values may be sent and summed in bfloat16 or wider, within the bound.
A program may use at most 64 MiB of HBM per device.

v0:
```python
import math

import jax
import jax.numpy as jnp
from jax import lax
from jax.sharding import PartitionSpec as P

HEAD_SIZE = 128
QSCALE = 168
WINDOW = 1024
REACH = 8


def passed_along(array, axis, by):
    peers = lax.axis_size(axis)
    pairs = [(i, i + by) for i in range(peers) if 0 <= i + by < peers]
    return lax.ppermute(array, axis, pairs)


def rotary_normed(unrotated_rows, gain_vec, token_positions, head_count):
    tokens_here = unrotated_rows.shape[0]
    entries = unrotated_rows.reshape(tokens_here, head_count, HEAD_SIZE)
    mean_sq = jnp.mean(entries * entries, axis=-1, keepdims=True)
    normed = entries * lax.rsqrt(mean_sq + 1e-06) * gain_vec
    half_dim = HEAD_SIZE // 2
    frequency = jnp.exp(jnp.arange(half_dim).astype(jnp.float32) * (-math.log(10000.0) / half_dim))
    angles = token_positions.astype(jnp.float32)[:, None] * frequency[None, :]
    cosine = jnp.cos(angles)[:, None, :]
    sine_part = jnp.sin(angles)[:, None, :]
    first_half = normed[..., :half_dim]
    second_half = normed[..., half_dim:]
    return jnp.concatenate(
        [
            first_half * cosine - second_half * sine_part,
            second_half * cosine + first_half * sine_part,
        ],
        axis=-1,
    )


def attend(query_blk, key_blk, value_blk, dattn_blk, visible):
    scale = float(QSCALE) ** (-0.5)
    scores = (
        jnp.einsum("qhgd,chd->hgqc", query_blk, key_blk, preferred_element_type=jnp.float32) * scale
    )
    scores = jnp.where(visible[None, None], scores, -jnp.inf)
    top_score = jnp.max(scores, axis=-1, keepdims=True)
    expd = jnp.exp(scores - top_score)
    probs = expd / jnp.sum(expd, axis=-1, keepdims=True)
    probs_b = probs.astype(jnp.bfloat16)
    dprobs = jnp.einsum("qhgd,chd->hgqc", dattn_blk, value_blk, preferred_element_type=jnp.float32)
    delta = jnp.sum(probs * dprobs, axis=-1, keepdims=True)
    dscores = (probs * (dprobs - delta)).astype(jnp.bfloat16)
    dquery = (
        jnp.einsum("hgqc,chd->qhgd", dscores, key_blk, preferred_element_type=jnp.float32) * scale
    )
    dkey = (
        jnp.einsum("hgqc,qhgd->chd", dscores, query_blk, preferred_element_type=jnp.float32) * scale
    )
    value_grad = jnp.einsum(
        "hgqc,qhgd->chd", probs_b, dattn_blk, preferred_element_type=jnp.float32
    )
    return (dquery, dkey, value_grad)


def on_device(
    layer_input,
    grad_out,
    doc_start,
    w_query,
    key_weight,
    value_weight,
    w_out,
    q_gain,
    key_norm_gain,
):
    tok_rows = layer_input.shape[0]
    full_query, full_key, full_value = (
        lax.all_gather(w_query, "seq", axis=0, tiled=True),
        lax.all_gather(key_weight, "seq", axis=0, tiled=True),
        lax.all_gather(value_weight, "seq", axis=0, tiled=True),
    )
    query_heads = full_query.shape[1] // HEAD_SIZE
    kv_heads = full_key.shape[1] // HEAD_SIZE
    group_width = query_heads // kv_heads
    seq_index = lax.axis_index("seq")
    token_index = seq_index * tok_rows + jnp.arange(tok_rows, dtype=jnp.int32)
    token_positions = token_index - doc_start
    query_raw = jnp.dot(layer_input, full_query, preferred_element_type=jnp.float32)
    key_unrotated = jnp.dot(layer_input, full_key, preferred_element_type=jnp.float32)
    value_row_matrix = jnp.dot(layer_input, full_value, preferred_element_type=jnp.float32).astype(
        jnp.bfloat16
    )
    query_full, query_back = jax.vjp(
        lambda unrotated_rows: rotary_normed(unrotated_rows, q_gain, token_positions, query_heads),
        query_raw,
    )
    key_complete, key_backward = jax.vjp(
        lambda unrotated_rows: rotary_normed(
            unrotated_rows, key_norm_gain, token_positions, kv_heads
        ),
        key_unrotated,
    )
    query_row_matrix = query_full.astype(jnp.bfloat16)
    key_row_matrix = key_complete.astype(jnp.bfloat16)
    attention_grad = lax.dot_general(
        grad_out,
        lax.all_gather(w_out, "seq", axis=1, tiled=True),
        (((1,), (1,)), ((), ())),
        preferred_element_type=jnp.float32,
    ).astype(jnp.bfloat16)
    key_value = jnp.stack(
        [key_row_matrix.reshape(tok_rows, kv_heads * HEAD_SIZE), value_row_matrix]
    )
    earlier = [key_value]
    for distance in range(1, REACH + 1):
        earlier.append(passed_along(key_value, "seq", distance))
    context = jnp.concatenate([earlier[distance] for distance in range(REACH, -1, -1)], axis=1)
    context_len = context.shape[1]
    key_index = (seq_index - REACH) * tok_rows + jnp.arange(context_len, dtype=jnp.int32)
    visible = (
        (key_index[None, :] >= doc_start[:, None])
        & (key_index[None, :] <= token_index[:, None])
        & (token_index[:, None] - key_index[None, :] < WINDOW)
    )
    dquery, dkey, value_grad = attend(
        query_row_matrix.reshape(tok_rows, kv_heads, group_width, HEAD_SIZE),
        context[0].reshape(context_len, kv_heads, HEAD_SIZE),
        context[1].reshape(context_len, kv_heads, HEAD_SIZE),
        attention_grad.reshape(tok_rows, kv_heads, group_width, HEAD_SIZE),
        visible,
    )
    key_grads = jnp.stack(
        [
            dkey.reshape(context_len, kv_heads * HEAD_SIZE),
            value_grad.reshape(context_len, kv_heads * HEAD_SIZE),
        ]
    )

    def block_of(distance):
        first_row = (REACH - distance) * tok_rows
        return key_grads[:, first_row : first_row + tok_rows]

    owned_grads = block_of(0)
    for distance in range(1, REACH + 1):
        owned_grads = owned_grads + passed_along(block_of(distance), "seq", -distance)
    key_total = owned_grads[0].reshape(tok_rows, kv_heads, HEAD_SIZE)
    value_total = owned_grads[1]
    dquery_raw = query_back(dquery.reshape(tok_rows, query_heads, HEAD_SIZE))[0].astype(
        jnp.bfloat16
    )
    dkey_raw = key_backward(key_total)[0].astype(jnp.bfloat16)
    dvalue_rows = value_total.astype(jnp.bfloat16)
    squares = jnp.square(layer_input.astype(jnp.float32))
    value_sq = value_total * value_total
    all_tokens = lax.axis_size("seq") * tok_rows
    fisher_term = lax.dot_general(
        squares,
        value_sq,
        (((0,), (0,)), ((), ())),
        precision=lax.Precision.HIGHEST,
        preferred_element_type=jnp.float32,
    )
    fisher_value = (
        lax.psum_scatter(fisher_term, "seq", scatter_dimension=0, tiled=True) / all_tokens
    )
    contract = (((1,), (1,)), ((), ()))
    total = lax.dot_general(dquery_raw, full_query, contract, preferred_element_type=jnp.float32)
    total = total + lax.dot_general(
        dkey_raw, full_key, contract, preferred_element_type=jnp.float32
    )
    grad_input = lax.psum_scatter(
        total
        + lax.dot_general(dvalue_rows, full_value, contract, preferred_element_type=jnp.float32),
        "head",
        scatter_dimension=0,
        tiled=True,
    ).astype(jnp.bfloat16)
    return (fisher_value, grad_input)


def solution(mesh):
    in_specs = (
        P("seq", None),
        P("seq", None),
        P("seq"),
        P("seq", "head"),
        P("seq", "head"),
        P("seq", "head"),
        P("head", "seq"),
        P(),
        P(),
    )
    out_specs = (P("seq", "head"), P(("seq", "head"), None))
    return jax.shard_map(
        on_device, mesh=mesh, in_specs=in_specs, out_specs=out_specs, check_vma=False
    )
```

profile of v0, /device:TPU:6, one launch (start us, length us, event | category | flops | bytes accessed | tf_op | source)
XLA Modules:
  0.0 1409.6 jit_solution(520456489507171597)
XLA Ops:
  11.1 202.9 %all-gather.11.cloned.1.call-done = bf16[128,21,256]{2,1,0:T(8,128)(2,1)} async-done(((bf16[1,21,256]{2,1,0:T(8,128)(2,1)}), bf16[128,21,256]{2,1,0:T(8,128)(2,1)}) %all-gather.11.cloned.1.call-update) | async-done | bytes 1376272 | tf_op jit(solution)/shard_map/all_gather | solution.py:80
  218.2 192.9 %all-gather.13.cloned.1.call-done = bf16[128,21,256]{2,1,0:T(8,128)(2,1)} async-done(((bf16[1,21,256]{2,1,0:T(8,128)(2,1)}), bf16[128,21,256]{2,1,0:T(8,128)(2,1)}) %all-gather.13.cloned.1.call-update) | async-done | bytes 1376272 | tf_op jit(solution)/shard_map/all_gather | solution.py:81
  413.9 5.5 collective-permute-start.1
  419.5 4.0 collective-permute-start
  426.3 4.5 collective-permute-start.6
  430.8 4.0 collective-permute-start.5
  434.8 5.3 collective-permute-start.2
  442.1 7.6 collective-permute-done.2
  454.0 6.3 collective-permute-done.4
  463.3 167.0 %all-gather.15.cloned.1.call-done = bf16[128,21,512]{2,1,0:T(8,128)(2,1)} async-done(((bf16[1,21,512]{2,1,0:T(8,128)(2,1)}), bf16[128,21,512]{2,1,0:T(8,128)(2,1)}) %all-gather.15.cloned.1.call-update) | async-done | bytes 2752528 | tf_op jit(solution)/shard_map/all_gather | solution.py:108
  630.4 3.9 reshape.228
  637.1 211.3 %all-gather.9.cloned.1.call-done = bf16[128,21,512]{2,1,0:T(8,128)(2,1)} async-done(((bf16[1,21,512]{2,1,0:T(8,128)(2,1)}), bf16[128,21,512]{2,1,0:T(8,128)(2,1)}) %all-gather.9.cloned.1.call-update) | async-done | bytes 2752528 | tf_op jit(solution)/shard_map/all_gather | solution.py:79
  848.4 3.9 reshape.222
  888.9 7.6 collective-permute-start.8
  905.8 4.6 collective-permute-start.12
  912.0 5.4 collective-permute-start.13
  925.5 17.2 %collective-permute-done.11 = f32[2,128,256]{1,2,0:T(8,128)S(1)} collective-permute-done((f32[2,128,256]{1,2,0:T(8,128)}, f32[2,128,256]{1,2,0:T(8,128)S(1)}, u32[]{:S(2)}, u32[]{:S(2)}) %collective-permute-start.11) | collective-permute-done | bytes 262176 | tf_op jit(solution)/shard_map/ppermute | solution.py:17
  942.7 4.0 collective-permute-done.12
  949.5 5.2 collective-permute-done.15
  956.5 3.9 fusion.7
  972.7 372.3 %fusion = f32[24,256]{1,0:T(8,128)S(1)} fusion(f32[2688,256]{1,0:T(8,128)S(1)} %copy-done.7), kind=kCustom, calls=%all-reduce-scatter | all-reduce-scatter fusion | flops 786433 | bytes 2779136
  1359.9 5.1 collective-permute-start.25
  1380.2 4.5 collective-permute-start.18
  1391.4 5.1 collective-permute-done.17
  (192 shorter events, 140.3 us)
Async XLA Ops:
  7.2 206.8 %all-gather.11.cloned.1.call-start = ((), (), s32[]{:S(2)}) async-start(), calls=%async_computation.3 | async-start | bytes 1585152 | tf_op jit(solution)/shard_map/all_gather | solution.py:80
  7.9 403.2 %all-gather.13.cloned.1.call-start = ((), (), s32[]{:S(2)}) async-start(), calls=%async_computation.4 | async-start | bytes 1585152 | tf_op jit(solution)/shard_map/all_gather | solution.py:81
  8.7 621.7 %all-gather.15.cloned.1.call-start = ((), (), s32[]{:S(2)}) async-start(), calls=%async_computation.5 | async-start | bytes 3170304 | tf_op jit(solution)/shard_map/all_gather | solution.py:108
  9.4 839.0 %all-gather.9.cloned.1.call-start = ((), (), s32[]{:S(2)}) async-start(), calls=%async_computation.2 | async-start | bytes 3170304 | tf_op jit(solution)/shard_map/all_gather | solution.py:79
  10.0 1391.5 %reduce-scatter.4.cloned.1.call-start = ((), (), s32[]{:S(2)}) async-start(), calls=%async_computation.1 | async-start | bytes 1720320 | tf_op jit(solution)/shard_map/reduce_scatter | solution.py:172
  413.9 26.2 %collective-permute-start.1 = (bf16[2,128,256]{2,1,0:T(8,128)(2,1)S(1)}, bf16[2,128,256]{2,1,0:T(8,128)(2,1)S(1)}, u32[]{:S(2)}, u32[]{:S(2)}) collective-permute-start(bf16[2,128,256]{2,1,0:T(8,128)(2,1)S(1)} %pad_maximum_fusion.2), channel_id=1, source_target_pairs={{0,28},{4,32},{8,36},{12,40},{16,44},{20,48},{24,52},{28,56},{32,6... | collective-permute-start | bytes 393224 | tf_op jit(solution)/shard_map/ppermute | solution.py:17
  419.5 15.3 %collective-permute-start = (bf16[2,128,256]{2,1,0:T(8,128)(2,1)S(1)}, bf16[2,128,256]{2,1,0:T(8,128)(2,1)S(1)}, u32[]{:S(2)}, u32[]{:S(2)}) collective-permute-start(bf16[2,128,256]{2,1,0:T(8,128)(2,1)S(1)} %pad_maximum_fusion.2), channel_id=1, source_target_pairs={{0,32},{4,36},{8,40},{12,44},{16,48},{20,52},{24,56},{28,60},{32,6... | collective-permute-start | bytes 393224 | tf_op jit(solution)/shard_map/ppermute | solution.py:17
  424.4 35.9 %collective-permute-start.7 = (bf16[2,128,256]{2,1,0:T(8,128)(2,1)S(1)}, bf16[2,128,256]{2,1,0:T(8,128)(2,1)S(1)}, u32[]{:S(2)}, u32[]{:S(2)}) collective-permute-start(bf16[2,128,256]{2,1,0:T(8,128)(2,1)S(1)} %pad_maximum_fusion.2), channel_id=1, source_target_pairs={{0,4},{4,8},{8,12},{12,16},{16,20},{20,24},{24,28},{28,32},{32,36}... | collective-permute-start | bytes 393224 | tf_op jit(solution)/shard_map/ppermute | solution.py:17
  426.3 34.0 %collective-permute-start.6 = (bf16[2,128,256]{2,1,0:T(8,128)(2,1)S(1)}, bf16[2,128,256]{2,1,0:T(8,128)(2,1)S(1)}, u32[]{:S(2)}, u32[]{:S(2)}) collective-permute-start(bf16[2,128,256]{2,1,0:T(8,128)(2,1)S(1)} %pad_maximum_fusion.2), channel_id=1, source_target_pairs={{0,8},{4,12},{8,16},{12,20},{16,24},{20,28},{24,32},{28,36},{32,40... | collective-permute-start | bytes 393224 | tf_op jit(solution)/shard_map/ppermute | solution.py:17
  430.8 29.5 %collective-permute-start.5 = (bf16[2,128,256]{2,1,0:T(8,128)(2,1)S(1)}, bf16[2,128,256]{2,1,0:T(8,128)(2,1)S(1)}, u32[]{:S(2)}, u32[]{:S(2)}) collective-permute-start(bf16[2,128,256]{2,1,0:T(8,128)(2,1)S(1)} %pad_maximum_fusion.2), channel_id=1, source_target_pairs={{0,12},{4,16},{8,20},{12,24},{16,28},{20,32},{24,36},{28,40},{32,4... | collective-permute-start | bytes 393224 | tf_op jit(solution)/shard_map/ppermute | solution.py:17
  888.9 23.1 %collective-permute-start.8 = (f32[2,128,256]{1,2,0:T(8,128)}, f32[2,128,256]{1,2,0:T(8,128)}, u32[]{:S(2)}, u32[]{:S(2)}) collective-permute-start(f32[2,128,256]{1,2,0:T(8,128)} %get-tuple-element.2), channel_id=1, source_target_pairs={{4,0},{8,4},{12,8},{16,12},{20,16},{24,20},{28,24},{32,28},{36,32}... | collective-permute-start | bytes 786440 | tf_op jit(solution)/shard_map/ppermute | solution.py:17
  896.6 20.9 %collective-permute-start.9 = (f32[2,128,256]{1,2,0:T(8,128)}, f32[2,128,256]{1,2,0:T(8,128)}, u32[]{:S(2)}, u32[]{:S(2)}) collective-permute-start(f32[2,128,256]{1,2,0:T(8,128)} %get-tuple-element.3), channel_id=1, source_target_pairs={{8,0},{12,4},{16,8},{20,12},{24,16},{28,20},{32,24},{36,28},{40,32... | collective-permute-start | bytes 786440 | tf_op jit(solution)/shard_map/ppermute | solution.py:17
  899.2 22.0 %collective-permute-start.10 = (f32[2,128,256]{1,2,0:T(8,128)}, f32[2,128,256]{1,2,0:T(8,128)}, u32[]{:S(2)}, u32[]{:S(2)}) collective-permute-start(f32[2,128,256]{1,2,0:T(8,128)} %get-tuple-element.4), channel_id=1, source_target_pairs={{12,0},{16,4},{20,8},{24,12},{28,16},{32,20},{36,24},{40,28},{44,3... | collective-permute-start | bytes 786440 | tf_op jit(solution)/shard_map/ppermute | solution.py:17
  902.9 39.8 %collective-permute-start.11 = (f32[2,128,256]{1,2,0:T(8,128)}, f32[2,128,256]{1,2,0:T(8,128)S(1)}, u32[]{:S(2)}, u32[]{:S(2)}) collective-permute-start(f32[2,128,256]{1,2,0:T(8,128)} %get-tuple-element.5), channel_id=1, source_target_pairs={{16,0},{20,4},{24,8},{28,12},{32,16},{36,20},{40,24},{44,28},{48,3... | collective-permute-start | bytes 786440 | tf_op jit(solution)/shard_map/ppermute | solution.py:17
  905.8 41.0 %collective-permute-start.12 = (f32[2,128,256]{1,2,0:T(8,128)}, f32[2,128,256]{1,2,0:T(8,128)S(1)}, u32[]{:S(2)}, u32[]{:S(2)}) collective-permute-start(f32[2,128,256]{1,2,0:T(8,128)} %get-tuple-element.6), channel_id=1, source_target_pairs={{20,0},{24,4},{28,8},{32,12},{36,16},{40,20},{44,24},{48,28},{52,3... | collective-permute-start | bytes 786440 | tf_op jit(solution)/shard_map/ppermute | solution.py:17
  912.0 37.5 %collective-permute-start.13 = (f32[2,128,256]{1,2,0:T(8,128)}, f32[2,128,256]{1,2,0:T(8,128)S(1)}, u32[]{:S(2)}, u32[]{:S(2)}) collective-permute-start(f32[2,128,256]{1,2,0:T(8,128)} %get-tuple-element.7), channel_id=1, source_target_pairs={{24,0},{28,4},{32,8},{36,12},{40,16},{44,20},{48,24},{52,28},{56,3... | collective-permute-start | bytes 786440 | tf_op jit(solution)/shard_map/ppermute | solution.py:17
  917.5 37.2 %collective-permute-start.15 = (f32[2,128,256]{1,2,0:T(8,128)}, f32[2,128,256]{1,2,0:T(8,128)S(1)}, u32[]{:S(2)}, u32[]{:S(2)}) collective-permute-start(f32[2,128,256]{1,2,0:T(8,128)} %get-tuple-element.8), channel_id=1, source_target_pairs={{32,0},{36,4},{40,8},{44,12},{48,16},{52,20},{56,24},{60,28},{64,3... | collective-permute-start | bytes 786440 | tf_op jit(solution)/shard_map/ppermute | solution.py:17
  921.2 34.0 %collective-permute-start.14 = (f32[2,128,256]{1,2,0:T(8,128)}, f32[2,128,256]{1,2,0:T(8,128)S(1)}, u32[]{:S(2)}, u32[]{:S(2)}) collective-permute-start(f32[2,128,256]{1,2,0:T(8,128)} %get-tuple-element.9), channel_id=1, source_target_pairs={{28,0},{32,4},{36,8},{40,12},{44,16},{48,20},{52,24},{56,28},{60,3... | collective-permute-start | bytes 786440 | tf_op jit(solution)/shard_map/ppermute | solution.py:17
  1348.9 16.1 %collective-permute-start.29 = (f32[24,256]{1,0:T(8,128)S(1)}, f32[24,256]{1,0:T(8,128)S(1)}, u32[]{:S(2)}, u32[]{:S(2)}) collective-permute-start(f32[24,256]{1,0:T(8,128)S(1)} %fusion), channel_id=1, source_target_pairs={{0,56},{4,60},{8,64},{12,68},{16,72},{20,76},{24,80},{28,84},{32,8... | collective-permute-start | bytes 73736
  1350.8 16.1 %collective-permute-start.28 = (f32[24,256]{1,0:T(8,128)S(1)}, f32[24,256]{1,0:T(8,128)S(1)}, u32[]{:S(2)}, u32[]{:S(2)}) collective-permute-start(f32[24,256]{1,0:T(8,128)S(1)} %fusion), channel_id=1, source_target_pairs={{0,52},{4,56},{8,60},{12,64},{16,68},{20,72},{24,76},{28,80},{32,8... | collective-permute-start | bytes 73736
  1352.7 16.1 %collective-permute-start.27 = (f32[24,256]{1,0:T(8,128)S(1)}, f32[24,256]{1,0:T(8,128)S(1)}, u32[]{:S(2)}, u32[]{:S(2)}) collective-permute-start(f32[24,256]{1,0:T(8,128)S(1)} %fusion), channel_id=1, source_target_pairs={{0,48},{4,52},{8,56},{12,60},{16,64},{20,68},{24,72},{28,76},{32,8... | collective-permute-start | bytes 73736
  1357.1 15.5 %collective-permute-start.26 = (f32[24,256]{1,0:T(8,128)S(1)}, f32[24,256]{1,0:T(8,128)S(1)}, u32[]{:S(2)}, u32[]{:S(2)}) collective-permute-start(f32[24,256]{1,0:T(8,128)S(1)} %fusion), channel_id=1, source_target_pairs={{0,44},{4,48},{8,52},{12,56},{16,60},{20,64},{24,68},{28,72},{32,7... | collective-permute-start | bytes 73736
  1368.9 15.8 %collective-permute-start.22 = (f32[24,256]{1,0:T(8,128)S(1)}, f32[24,256]{1,0:T(8,128)S(1)}, u32[]{:S(2)}, u32[]{:S(2)}) collective-permute-start(f32[24,256]{1,0:T(8,128)S(1)} %fusion), channel_id=1, source_target_pairs={{0,28},{4,32},{8,36},{12,40},{16,44},{20,48},{24,52},{28,56},{32,6... | collective-permute-start | bytes 73736
  1374.8 16.5 %collective-permute-start.20 = (f32[24,256]{1,0:T(8,128)S(1)}, f32[24,256]{1,0:T(8,128)S(1)}, u32[]{:S(2)}, u32[]{:S(2)}) collective-permute-start(f32[24,256]{1,0:T(8,128)S(1)} %fusion), channel_id=1, source_target_pairs={{0,20},{4,24},{8,28},{12,32},{16,36},{20,40},{24,44},{28,48},{32,5... | collective-permute-start | bytes 73736
  (40 other events, 1778.9 us)
Sparse Core Ops, SparseCore 0:
  12.3 201.6 all-gather.10
  218.2 192.8 all-gather.12
  415.7 214.6 all-gather.14
  634.8 213.6 all-gather.8
  972.3 24.6 reduce-scatter.3
where the time goes:
time: 1420 us; the launch traced here: 1410 us
  waiting for transfers between devices  833 us (59%)
  blocking collectives  372 us (26%)
  starting transfers between devices  102 us (7%)
  local copies, waits for them, and re-layouts  40 us (3%)
  matrix products  24.2 us (2%)
  other arithmetic  22.4 us (2%)
  between operations  15.4 us (1%)
    unnamed x1, blocking collectives  372 us
    all_gather x1, waiting for transfers between devices, on_device(): lax.all_gather(w_query, 'seq', axis=0, tiled=True)  211 us
    all_gather x1, waiting for transfers between devices, on_device(): lax.all_gather(key_weight, 'seq', axis=0, tiled=True)  203 us
    all_gather x1, waiting for transfers between devices, on_device(): lax.all_gather(value_weight, 'seq', axis=0, tiled=True)  193 us
    all_gather x1, waiting for transfers between devices, on_device(): lax.all_gather(w_out, 'seq', axis=1, tiled=True)  167 us
    ppermute x16, starting transfers between devices, passed_along(): return lax.ppermute(array, axis, pairs)  61.4 us
    ppermute x16, waiting for transfers between devices, passed_along(): return lax.ppermute(array, axis, pairs)  45.4 us
    unnamed x16, starting transfers between devices  40.3 us
  transfers between devices with their start and end apart: 37, of which 17 were waited for; matrix products, arithmetic and copies ran while one was open for 28% of the time, Pallas kernels for 0%

commit v1 on v0

v1 whole, which is shorter than its diff:
```python
import math

import jax
import jax.numpy as jnp
from jax import lax
from jax.experimental import pallas as pl
from jax.experimental.pallas import tpu as pltpu
from jax.sharding import PartitionSpec as P

HEAD_SIZE = 128
QSCALE = 168
WINDOW = 1024
NH, NZ, NY, NHEAD = 2, 16, 4, 4
SEQ = NH * NZ * NY
TOK = 128
WIDTH = 2688
ROWS = WIDTH // SEQ
SLOT = 64
FSLOT = 48
GROUP = 16
SPAN = GROUP * ROWS
WIN = 512
F32 = jnp.float32
BF16 = jnp.bfloat16


def dot(a, b, ca=1, cb=0):
    return lax.dot_general(a, b, (((ca,), (cb,)), ((), ())), preferred_element_type=F32)


def iota(shape, axis):
    return lax.broadcasted_iota(jnp.int32, shape, axis)


def rotary(normed, cosine, sine):
    return normed * cosine + pltpu.roll(normed, HEAD_SIZE // 2, 1) * sine


def norm_forward(raw, gain, cosine, sine):
    inv = lax.rsqrt(jnp.mean(raw * raw, axis=1, keepdims=True) + 1e-06)
    return rotary(raw * inv * gain, cosine, sine)


def norm_backward(grad, raw, gain, cosine, sine):
    inv = lax.rsqrt(jnp.mean(raw * raw, axis=1, keepdims=True) + 1e-06)
    back = (grad * cosine + pltpu.roll(grad * sine, HEAD_SIZE // 2, 1)) * gain
    along = jnp.mean(raw * back, axis=1, keepdims=True)
    return inv * (back - raw * (inv * inv * along))


def body(
    piece, x_ref, g_ref, start_ref, cos_ref, sin_ref, qg_ref, kg_ref,
    gi_ref, fv_ref,
    full, lhs, acc, ctx, dctx, ret, tree, treeback, qn, dqn, total, parts, arrived,
    fpad, fone, ftwo, fsend, fy, zsend, zrecv, hsend, hrecv, kvraw,
    send_sem, recv_sem, local_sem,
):
    s = lax.axis_index("seq")
    hd = lax.axis_index("head")
    h = s // (NZ * NY)
    z = lax.rem(s // NY, NZ)
    y = lax.rem(s, NY)
    base = h * (NZ * NY)

    def at_z(step):
        return base + lax.rem(z + step + NZ, NZ) * NY + y

    def at_y(step):
        return base + z * NY + lax.rem(y + step + NY, NY)

    def shifted(step):
        return lax.rem(s + step + SEQ, SEQ)

    zi = lambda step: lax.rem(z + step + 2 * NZ, NZ)
    yi = lambda step: lax.rem(y + step + NY, NY)
    across = (1 - h) * (NZ * NY) + z * NY + y

    barrier = pltpu.get_barrier_semaphore()
    seq_partners = [at_z(1), at_z(-1), at_y(1), at_y(2), at_y(3), across]
    seq_partners += [shifted(4), shifted(-4), shifted(8), shifted(-8)]
    for partner in seq_partners:
        pl.semaphore_signal(barrier, inc=1, device_id={"seq": partner})
    for e in range(1, NHEAD):
        pl.semaphore_signal(barrier, inc=1, device_id={"head": lax.rem(hd + e, NHEAD)})
    pl.semaphore_wait(barrier, len(seq_partners) + NHEAD - 1)

    def remote(src, dst, sem, target, axis="seq"):
        return pltpu.make_async_remote_copy(
            src_ref=src,
            dst_ref=dst,
            send_sem=send_sem.at[sem],
            recv_sem=recv_sem.at[sem],
            device_id={axis: target},
        )

    def here(dst, sem):
        return remote(dst, dst, sem, across)

    HX = 0
    AZ = 1
    BZ = AZ + 16
    AY = BZ + 16
    BY = AY + 64
    KV = BY + 4
    DK = KV + 8
    GR = DK + 8
    FY = GR + 3
    FZ = FY + 6
    FH = FZ + 16

    def rows(lo, n):
        return pl.ds(lo, n)

    def a_piece(zz, yy, lo, n):
        return full.at[:, zz, yy, rows(lo, n), :]

    def b_piece(zz, lo, n):
        return full.at[:, zz, :, rows(lo, n), :]

    def az(k, side, last=False):
        zz = zi(-(k - 1)) if side == 0 else zi(k - 1)
        ref = a_piece(zz, y, 16 * side if last else 0, 16 if last else 32)
        return remote(ref, ref, AZ + 2 * (k - 1) + side, at_z(1 if side == 0 else -1))

    def az_in(k, side, last=False):
        zz = zi(-k) if side == 0 else zi(k)
        ref = a_piece(zz, y, 16 * side if last else 0, 16 if last else 32)
        return here(ref, AZ + 2 * (k - 1) + side)

    def bz(k, side, last=False):
        zz = zi(-(k - 1)) if side == 0 else zi(k - 1)
        ref = b_piece(zz, 32 + 16 * side if last else 32, 16 if last else 32)
        return remote(ref, ref, BZ + 2 * (k - 1) + side, at_z(1 if side == 0 else -1))

    def bz_in(k, side, last=False):
        zz = zi(-k) if side == 0 else zi(k)
        ref = b_piece(zz, 32 + 16 * side if last else 32, 16 if last else 32)
        return here(ref, BZ + 2 * (k - 1) + side)

    def ring_y(zz, sem, lo):
        own = a_piece(zz, y, lo, 32)
        first = [
            remote(own, own, sem, at_y(1)),
            remote(own, own, sem + 1, at_y(3)),
        ]
        left, right, far = yi(3), yi(1), yi(2)
        first_in = [
            here(a_piece(zz, left, lo, 32), sem),
            here(a_piece(zz, right, lo, 32), sem + 1),
        ]
        up = a_piece(zz, left, lo, 16)
        down = a_piece(zz, right, lo + 16, 16)
        second = [
            remote(up, up, sem + 2, at_y(1)),
            remote(down, down, sem + 3, at_y(3)),
        ]
        second_in = [
            here(a_piece(zz, far, lo, 16), sem + 2),
            here(a_piece(zz, far, lo + 16, 16), sem + 3),
        ]
        return first, first_in, second, second_in

    def ay(step, index):
        return ring_y(zi(step), AY + 4 * index, 0)

    def ay_start(step, index):
        for copy in ay(step, index)[0]:
            copy.start()

    def ay_forward(step, index):
        first, first_in, second, second_in = ay(step, index)
        for side in range(2):
            first_in[side].wait_recv()
            second[side].start()

    def ay_finish(step, index):
        first, first_in, second, second_in = ay(step, index)
        for side in range(2):
            second_in[side].wait_recv()
            first[side].wait_send()
            second[side].wait_send()

    own_slot = full.at[h, z, y]
    cross = remote(piece, own_slot, HX, across)
    cross.start()
    keep = pltpu.make_async_copy(piece, own_slot, local_sem.at[0])
    keep.start()
    keep.wait()
    here(full.at[1 - h, z, y], HX).wait_recv()

    b_first, b_first_in, b_second, b_second_in = ring_y(z, BY, 32)
    for side in range(2):
        b_first[side].start()
    for side in range(2):
        az(1, side).start()
    ay_start(0, 0)
    for side in range(2):
        b_first_in[side].wait_recv()
        b_second[side].start()

    def selection(j):
        first_row = SPAN * j
        low = jnp.minimum((first_row // 128) * 128, WIDTH - WIN)
        return pl.multiple_of(low, 128), first_row - low

    def prepare(j):
        low, offset = selection(j)
        column = iota((1, GROUP * SLOT), 1)
        slot = column & (SLOT - 1)
        target = jnp.where(slot < ROWS, offset + (column >> 6) * ROWS + slot, -1)
        select = jnp.where(iota((WIN, GROUP * SLOT), 0) == target, 1.0, 0.0).astype(BF16)
        spread = dot(x_ref[:, pl.ds(low, WIN)], select)
        lhs[j, 0:TOK] = spread.astype(BF16)
        lhs[j, TOK : 2 * TOK] = pltpu.roll(spread, ROWS, 1).astype(BF16)
        spread = dot(g_ref[:, pl.ds(low, WIN)], select)
        lhs[j, 2 * TOK :] = pltpu.roll(spread, 2 * ROWS, 1).astype(BF16)

    prepare(0)
    for side in range(2):
        b_second_in[side].wait_recv()
    for side in range(2):
        bz(1, side).start()

    def step_of(k, last_z, last_next):
        for side in range(2):
            az_in(k, side, last_z).wait_recv()
            if not last_z:
                az(k + 1, side, last_next).start()
        if last_z:
            ay_start(8, 15)
        else:
            ay_start(-k, 2 * k - 1)
            ay_start(k, 2 * k)
        for side in range(2):
            bz_in(k, side, last_z).wait_recv()
            if not last_z:
                bz(k + 1, side, last_next).start()

    step_of(1, False, False)
    ay_forward(0, 0)
    prepare(1)

    def steps(k, carry):
        step_of(k, False, False)
        ay_forward(1 - k, 2 * k - 3)
        ay_forward(k - 1, 2 * k - 2)
        prepare(k)
        return carry

    lax.fori_loop(2, 7, steps, 0)
    step_of(7, False, True)
    ay_forward(-6, 11)
    ay_forward(6, 12)
    prepare(7)
    step_of(8, True, True)
    ay_forward(-7, 13)
    ay_forward(7, 14)
    ay_forward(8, 15)

    cross.wait_send()
    for side in range(2):
        b_first[side].wait_send()
        b_second[side].wait_send()
    for k in range(1, 9):
        for side in range(2):
            az(k, side, k == 8).wait_send()
            bz(k, side, k == 8).wait_send()
    ay_finish(0, 0)

    def finish(k, carry):
        ay_finish(-k, 2 * k - 1)
        ay_finish(k, 2 * k)
        return carry

    lax.fori_loop(1, 8, finish, 0)
    ay_finish(8, 15)

    def weights(j):
        return full[j // 4, pl.ds(4 * lax.rem(j, 4), 4)].reshape(GROUP * SLOT, 512)

    acc[...] = jnp.zeros_like(acc)

    def project(j, carry):
        acc[...] += dot(lhs[j], weights(j))
        return carry

    lax.fori_loop(0, SEQ // GROUP, project, 0)

    cosine, sine = cos_ref[...], sin_ref[...]
    q_gain, k_gain = qg_ref[...], kg_ref[...]
    for i in range(2):
        cols = slice(i * 128, (i + 1) * 128)
        ctx[0, 0, :, cols] = norm_forward(acc[0:TOK, cols], k_gain, cosine, sine).astype(BF16)
    ctx[0, 1] = acc[0:TOK, 256:512].astype(BF16)
    for i in range(4):
        cols = slice(i * 128, (i + 1) * 128)
        qn[i // 2, (i % 2) * TOK : (i % 2 + 1) * TOK] = norm_forward(
            acc[TOK : 2 * TOK, cols], q_gain, cosine, sine
        ).astype(BF16)

    hop4 = remote(ctx.at[0], ctx.at[4], KV, shifted(4))
    hop8 = remote(ctx.at[0], ctx.at[8], KV + 1, shifted(8))
    hop4.start()
    hop8.start()

    def side_copies(e):
        low = jnp.where(y + e < NY, 0, 4)
        one = remote(ctx.at[low], ctx.at[e], KV + 2 * e, at_y(e))
        two = remote(ctx.at[low + 4], ctx.at[e + 4], KV + 2 * e + 1, at_y(e))
        return one, two

    for e in range(1, NY):
        @pl.when(y + e < NY)
        def _():
            side_copies(e)[0].start()
    for i in range(4):
        cols = slice(i * 128, (i + 1) * 128)
        dqn[i // 2, (i % 2) * TOK : (i % 2 + 1) * TOK] = acc[2 * TOK :, cols].astype(BF16)
    here(ctx.at[4], KV).wait_recv()
    for e in range(1, NY):
        @pl.when(y + e < NY)
        def _():
            side_copies(e)[1].start()

        @pl.when(y + e >= NY)
        def _():
            side_copies(e)[0].start()
    here(ctx.at[8], KV + 1).wait_recv()
    for e in range(1, NY):
        @pl.when(y + e >= NY)
        def _():
            side_copies(e)[1].start()
    for e in range(1, NY):
        here(ctx.at[e], KV + 2 * e).wait_recv()
        here(ctx.at[e + 4], KV + 2 * e + 1).wait_recv()
    hop4.wait_send()
    hop8.wait_send()
    for e in range(1, NY):
        one, two = side_copies(e)
        one.wait_send()
        two.wait_send()

    scale = float(QSCALE) ** (-0.5)
    reach = 9 * TOK
    place = iota((reach, 1), 0)
    key_index = s * TOK - (place & ~(TOK - 1)) + (place & (TOK - 1))
    query_index = s * TOK + (iota((1, 2 * TOK), 1) & (TOK - 1))
    visible = (
        (key_index >= start_ref[...])
        & (key_index <= query_index)
        & (query_index - key_index < WINDOW)
    )
    for i in range(2):
        cols = slice(i * 128, (i + 1) * 128)
        keys = ctx[:, 0, :, cols].reshape(reach, 128)
        values = ctx[:, 1, :, cols].reshape(reach, 128)
        queries, douts = qn[i], dqn[i]
        scores = jnp.where(visible, dot(keys, queries, 1, 1) * scale, -jnp.inf)
        expd = jnp.exp(scores - jnp.max(scores, axis=0, keepdims=True))
        probs = expd * (1.0 / jnp.sum(expd, axis=0, keepdims=True))
        dprobs = dot(values, douts, 1, 1)
        delta = jnp.sum(probs * dprobs, axis=0, keepdims=True)
        dscores = (probs * (dprobs - delta)).astype(BF16)
        dctx[:, 0, :, cols] = (dot(dscores, queries) * scale).astype(BF16).reshape(9, TOK, 128)
        dctx[:, 1, :, cols] = dot(probs.astype(BF16), douts).astype(BF16).reshape(9, TOK, 128)
        dquery = dot(dscores, keys, 0, 0) * scale
        for r in range(2):
            col = slice((2 * i + r) * 128, (2 * i + r + 1) * 128)
            kvraw[0, :, col] = norm_backward(
                dquery[r * TOK : (r + 1) * TOK], acc[TOK : 2 * TOK, col], q_gain, cosine, sine
            ).astype(BF16)

    for e in range(1, NY):
        remote(dctx.at[e], ret.at[e - 1, 0], DK + 2 * e, at_y(NY - e)).start()
        remote(dctx.at[e + 4], ret.at[e - 1, 1], DK + 2 * e + 1, at_y(NY - e)).start()

    total[...] = jnp.zeros_like(total)

    def spread_back(which):
        low_slot = ROWS if which == 0 else 0

        def run(j, carry):
            low, offset = selection(j)
            out = dot(kvraw[which], weights(j), 1, 1).astype(BF16)
            row = iota((GROUP * SLOT, 1), 0)
            slot = (row & (SLOT - 1)) - low_slot
            target = jnp.where(
                (slot >= 0) & (slot < ROWS), offset + (row >> 6) * ROWS + slot, -1
            )
            select = jnp.where(iota((GROUP * SLOT, WIN), 1) == target, 1.0, 0.0).astype(BF16)
            total[:, pl.ds(low, WIN)] += dot(out, select)
            return carry

        lax.fori_loop(0, SEQ // GROUP, run, 0)

    sums = [dctx[4 * i].astype(F32) for i in range(3)]
    for e in range(1, NY):
        here(ret.at[e - 1, 0], DK + 2 * e).wait_recv()
        here(ret.at[e - 1, 1], DK + 2 * e + 1).wait_recv()
        same = y + e < NY
        one = ret[e - 1, 0].astype(F32)
        two = ret[e - 1, 1].astype(F32)
        sums[0] += jnp.where(same, one, 0.0)
        sums[1] += jnp.where(same, two, one)
        sums[2] += jnp.where(same, 0.0, two)
    tree[0] = sums[1].astype(BF16)
    tree[1] = sums[2].astype(BF16)
    back4 = remote(tree.at[0], treeback.at[0], DK, shifted(-4))
    back8 = remote(tree.at[1], treeback.at[1], DK + 1, shifted(-8))
    back4.start()
    back8.start()
    kvown = sums[0]
    spread_back(0)
    here(treeback.at[0], DK).wait_recv()
    here(treeback.at[1], DK + 1).wait_recv()
    kvgrad = kvown + treeback[0].astype(F32) + treeback[1].astype(F32)
    back4.wait_send()
    back8.wait_send()
    for e in range(1, NY):
        remote(dctx.at[e], ret.at[e - 1, 0], DK + 2 * e, at_y(NY - e)).wait_send()
        remote(dctx.at[e + 4], ret.at[e - 1, 1], DK + 2 * e + 1, at_y(NY - e)).wait_send()
    dvalue = kvgrad[1]

    place = iota((FSLOT, SPAN), 1)
    slot = iota((FSLOT, SPAN), 0)
    rank = jnp.where(slot < ROWS, slot, jnp.where(slot < 2 * ROWS, slot - ROWS, -WIDTH))
    select = jnp.concatenate(
        [jnp.where(place == rank + ROWS * i, 1.0, 0.0).astype(BF16) for i in range(GROUP)], axis=0
    )
    first_cols = jnp.where(iota((GROUP, FSLOT, 128), 1) < ROWS, 1.0, 0.0)
    dv_sq = (dvalue * dvalue).astype(BF16)

    def squares(i, carry):
        block = x_ref[:, pl.ds(pl.multiple_of(i * 384, 128), 384)].astype(F32)
        fone[pl.ds(pl.multiple_of(i * 384, 128), 384)] = dot(
            (block * block).astype(BF16), dv_sq, 0, 0
        ).astype(BF16)
        return carry

    lax.fori_loop(0, WIDTH // 384, squares, 0)

    def slots(j, carry):
        both = dot(select, fone[pl.ds(pl.multiple_of(SPAN * j, 16), SPAN)])
        both = both.reshape(GROUP, FSLOT, 256)
        picked = jnp.where(first_cols > 0.5, both[:, :, 0:128], both[:, :, 128:256])
        fpad[j // 4, pl.ds(4 * lax.rem(j, 4), 4)] = picked.astype(BF16).reshape(4, 4, FSLOT, 128)
        return carry

    lax.fori_loop(0, SEQ // GROUP, slots, 0)

    far, right, left = yi(2), yi(1), yi(3)
    f1 = remote(fpad.at[0, :, far], ftwo.at[0], FY, at_y(1))
    f2 = remote(fpad.at[1, :, far], ftwo.at[1], FY + 1, at_y(3))
    f3 = remote(fpad.at[1, :, right], ftwo.at[2], FY + 2, at_y(1))
    f4 = remote(fpad.at[0, :, left], ftwo.at[3], FY + 3, at_y(3))
    for copy in (f1, f2, f3, f4):
        copy.start()

    for i in range(2):
        cols = slice(i * 128, (i + 1) * 128)
        kvraw[1, :, cols] = norm_backward(
            kvgrad[0, :, cols], acc[0:TOK, cols], k_gain, cosine, sine
        ).astype(BF16)
    kvraw[1, :, 256:512] = dvalue.astype(BF16)

    here(ftwo.at[0], FY).wait_recv()
    fsend[0] = (fpad[0, :, right].astype(F32) + ftwo[0].astype(F32)).astype(BF16)
    f5 = remote(fsend.at[0], ftwo.at[4], FY + 4, at_y(1))
    f5.start()
    here(ftwo.at[1], FY + 1).wait_recv()
    fsend[1] = (fpad[1, :, left].astype(F32) + ftwo[1].astype(F32)).astype(BF16)
    f6 = remote(fsend.at[1], ftwo.at[5], FY + 5, at_y(3))
    f6.start()

    spread_back(1)
    for i in range(NHEAD):
        parts[i] = total[i * 32 : (i + 1) * 32].astype(BF16)
    shares = []
    for e in range(1, NHEAD):
        to = lax.rem(hd + e, NHEAD)
        shares.append(remote(parts.at[to], arrived.at[e - 1], GR + e - 1, to, "head"))
        shares[-1].start()

    for i in range(2, 6):
        here(ftwo.at[i], FY + i).wait_recv()
    fy[0] = fpad[0, :, y].astype(F32) + ftwo[4].astype(F32) + ftwo[3].astype(F32)
    fy[1] = fpad[1, :, y].astype(F32) + ftwo[2].astype(F32) + ftwo[5].astype(F32)

    def fz(k, side, first=False):
        i = 2 * (k - 1) + side
        src, dst = zsend.at[i], zrecv.at[i]
        if first:
            src, dst = src.at[side], dst.at[side]
        return remote(src, dst, FZ + i, at_z(1 if side == 0 else -1))

    def fz_in(k, side, first=False):
        i = 2 * (k - 1) + side
        return here(zrecv.at[i].at[side] if first else zrecv.at[i], FZ + i)

    for side in range(2):
        zsend[side, side] = fy[side, zi(8)].astype(BF16)
        fz(1, side, True).start()
    for k in range(1, 8):
        for side in range(2):
            fz_in(k, side, k == 1).wait_recv()
            i = 2 * (k - 1) + side
            own = zi(8 - k) if side == 0 else zi(k - 8)
            for part in range(2):
                value = fy[part, own]
                if k > 1 or part == side:
                    value = value + zrecv[i, part].astype(F32)
                zsend[i + 2, part] = value.astype(BF16)
            fz(k + 1, side).start()
    for side in range(2):
        fz_in(8, side).wait_recv()
    sums = [fy[p, z] + zrecv[14, p].astype(F32) + zrecv[15, p].astype(F32) for p in range(2)]
    low_half = h == 0
    hsend[...] = jnp.where(low_half, sums[1], sums[0]).astype(BF16)
    last = remote(hsend, hrecv, FH, across)
    last.start()

    for e in range(1, NHEAD):
        here(arrived.at[e - 1], GR + e - 1).wait_recv()
    mine = total[pl.ds(pl.multiple_of(hd * 32, 32), 32)]
    for e in range(1, NHEAD):
        mine = mine + arrived[e - 1].astype(F32)
    gi_ref[...] = mine.astype(BF16)
    for copy in shares:
        copy.wait_send()

    here(hrecv, FH).wait_recv()
    fv_ref[...] = (jnp.where(low_half, sums[0], sums[1]) + hrecv[...].astype(F32)) * (
        1.0 / (SEQ * TOK)
    )
    last.wait_send()
    for copy in (f1, f2, f3, f4, f5, f6):
        copy.wait_send()
    for k in range(1, 9):
        for side in range(2):
            fz(k, side, k == 1).wait_send()


def layer(piece, x, g, starts, cosine, sine, q_gain, k_gain):
    vmem = pl.BlockSpec(memory_space=pltpu.VMEM)
    sems = 160
    return pl.pallas_call(
        body,
        name="layer_backward",
        out_shape=(
            jax.ShapeDtypeStruct((32, WIDTH), BF16),
            jax.ShapeDtypeStruct((FSLOT, 128), F32),
        ),
        in_specs=[pl.BlockSpec(memory_space=pl.ANY)] + [vmem] * 7,
        out_specs=(vmem, vmem),
        scratch_shapes=[
            pltpu.VMEM((NH, NZ, NY, SLOT, 512), BF16),
            pltpu.VMEM((SEQ // GROUP, 3 * TOK, GROUP * SLOT), BF16),
            pltpu.VMEM((3 * TOK, 512), F32),
            pltpu.VMEM((9, 2, TOK, 256), BF16),
            pltpu.VMEM((9, 2, TOK, 256), BF16),
            pltpu.VMEM((3, 2, 2, TOK, 256), BF16),
            pltpu.VMEM((2, 2, TOK, 256), BF16),
            pltpu.VMEM((2, 2, TOK, 256), BF16),
            pltpu.VMEM((2, 2 * TOK, 128), BF16),
            pltpu.VMEM((2, 2 * TOK, 128), BF16),
            pltpu.VMEM((TOK, WIDTH), F32),
            pltpu.VMEM((NHEAD, 32, WIDTH), BF16),
            pltpu.VMEM((NHEAD - 1, 32, WIDTH), BF16),
            pltpu.VMEM((NH, NZ, NY, FSLOT, 128), BF16),
            pltpu.VMEM((WIDTH, 256), BF16),
            pltpu.VMEM((6, NZ, FSLOT, 128), BF16),
            pltpu.VMEM((2, NZ, FSLOT, 128), BF16),
            pltpu.VMEM((NH, NZ, FSLOT, 128), F32),
            pltpu.VMEM((16, NH, FSLOT, 128), BF16),
            pltpu.VMEM((16, NH, FSLOT, 128), BF16),
            pltpu.VMEM((FSLOT, 128), BF16),
            pltpu.VMEM((FSLOT, 128), BF16),
            pltpu.VMEM((2, TOK, 512), BF16),
            pltpu.SemaphoreType.DMA((sems,)),
            pltpu.SemaphoreType.DMA((sems,)),
            pltpu.SemaphoreType.DMA((1,)),
        ],
        compiler_params=pltpu.CompilerParams(
            collective_id=0, has_side_effects=True, vmem_limit_bytes=60 * 1024 * 1024
        ),
    )(piece, x, g, starts, cosine, sine, q_gain, k_gain)


def on_device(
    layer_input,
    grad_out,
    doc_start,
    w_query,
    key_weight,
    value_weight,
    w_out,
    q_gain,
    key_norm_gain,
):
    seq_index = lax.axis_index("seq")
    token_index = seq_index * TOK + jnp.arange(TOK, dtype=jnp.int32)
    positions = (token_index - doc_start).astype(F32)
    half = HEAD_SIZE // 2
    frequency = jnp.exp(jnp.arange(half).astype(F32) * (-math.log(10000.0) / half))
    angles = positions[:, None] * frequency[None, :]
    cosine, sine = jnp.cos(angles), jnp.sin(angles)
    cosine = jnp.concatenate([cosine, cosine], axis=1)
    sine = jnp.concatenate([-sine, sine], axis=1)
    piece = jnp.concatenate(
        [
            jnp.concatenate([key_weight, value_weight], axis=1),
            w_query,
            w_out.T,
            jnp.zeros((1, 512), BF16),
        ],
        axis=0,
    )
    starts = jnp.concatenate([doc_start, doc_start])[None, :]
    grad_input, sums = layer(
        piece, layer_input, grad_out, starts, cosine, sine, q_gain[None, :], key_norm_gain[None, :]
    )
    fisher_value = jnp.concatenate([sums[0:ROWS], sums[ROWS : 2 * ROWS]], axis=1)
    return (fisher_value, grad_input)


def solution(mesh):
    in_specs = (
        P("seq", None),
        P("seq", None),
        P("seq"),
        P("seq", "head"),
        P("seq", "head"),
        P("seq", "head"),
        P("head", "seq"),
        P(),
        P(),
    )
    out_specs = (P("seq", "head"), P(("seq", "head"), None))
    return jax.shard_map(
        on_device, mesh=mesh, in_specs=in_specs, out_specs=out_specs, check_vma=False
    )
```

time: 1420 us -> 190 us (0.13)
  waiting for transfers between devices: 833 us -> 0 us
  blocking collectives: 372 us -> 0 us
  Pallas kernels: 0 us -> 181 us
  starting transfers between devices: 102 us -> 0 us
  local copies, waits for them, and re-layouts: 40 us -> 2.48 us
  matrix products: 24.2 us -> 0 us
  other arithmetic: 22.4 us -> 5.11 us
  between operations: 15.4 us -> 0.66 us
    all_gather x4 -> x0, waiting for transfers between devices: 774 us -> none  [the longest x1 211 us: on_device(): lax.all_gather(w_query, 'seq', axis=0, tiled=True)]
    unnamed x1 -> x0, blocking collectives: 372 us -> none
    pallas_call x0 -> x1, Pallas kernels: none -> 181 us  [layer(): pl.pallas_call(body, name='layer_backward', out_shape=(jax.ShapeDtypeStru...]
    ppermute x16 -> x0, starting transfers between devices: 61.4 us -> none  [passed_along(): return lax.ppermute(array, axis, pairs)]
    ppermute x16 -> x0, waiting for transfers between devices: 45.4 us -> none  [passed_along(): return lax.ppermute(array, axis, pairs)]
    unnamed x16 -> x0, starting transfers between devices: 40.3 us -> none
    unnamed x73 -> x3, local copies, waits for them, and re-layouts: 27.2 us -> 1.6 us
    dot_general x12 -> x0, matrix products: 20.7 us -> none  [the longest x1 3.88 us: on_device(): lax.dot_general(squares, value_sq, (((0,), (0,)), ((), ())), precision=la...]
  transfers between devices with their start and end apart: 37 -> 0, of which waited for: 17 -> 0; matrix products, arithmetic and copies ran while one was open for 28% -> 0% of each run, Pallas kernels for 0% -> 0%
where the time goes in v1:
time: 190 us
  Pallas kernels  181 us (95%)
  other arithmetic  5.11 us (3%)
  local copies, waits for them, and re-layouts  2.48 us (1%)
    pallas_call x1, Pallas kernels, layer(): pl.pallas_call(body, name='layer_backward', out_shape=(jax.ShapeDtypeStru...  181 us

profile of v1, /device:TPU:6, one launch (start us, length us, event | category | flops | bytes accessed | tf_op | source)
XLA Modules:
  0.0 189.5 jit_solution(16499160597655644323)
XLA Ops:
  0.6 0.0 copy-start
  0.6 0.7 subtract_convert_fusion
  1.3 0.1 pad.12.clone
  1.4 1.3 pad_add_fusion
  2.7 0.0 copy-done
  2.7 1.4 maximum_maximum_fusion.piece
  4.1 0.3 fusion
  4.5 0.8 pad_maximum_fusion
  5.2 181.3 %layer_backward.1 = (bf16[32,2688]{1,0:T(8,128)(2,1)}, f32[48,128]{1,0:T(8,128)}) custom-call(bf16[64,512]{1,0:T(8,128)(2,1)} %maximum_maximum_fusion.piece, bf16[128,2688]{1,0:T(8,128)(2,1)} %x_ref.1, bf16[128,2688]{1,0:T(8,128)(2,1)} %g_ref.1, s32[1,256]{1,0:T(1,128)} %bitcast.6, f32[128,128]{1,0:T(8,128)} %get-tuple-element.11.cos_ref, ...), custom_call_target="tpu_custom_call" | custom-call | tf_op jit(solution)/shard_map/layer_backward/pallas_call | solution.py:546
  186.5 0.8 fusion.1
  187.3 0.6 pad_maximum_fusion.2
  187.9 1.6 copy.12
  (1 shorter events, 0.0 us)
Async XLA Ops:
  0.6 2.1 %copy-start = (bf16[512,21]{0,1:T(8,128)(2,1)S(1)}, bf16[512,21]{0,1:T(8,128)(2,1)}, u32[]{:S(2)}) copy-start(bf16[512,21]{0,1:T(8,128)(2,1)} %param.15) | copy-start | bytes 64516

commit v2 on v1

--- a/solution.py
+++ b/solution.py
@@ -52,7 +52,8 @@
     piece, x_ref, g_ref, start_ref, cos_ref, sin_ref, qg_ref, kg_ref,
     gi_ref, fv_ref,
     full, lhs, acc, ctx, dctx, ret, tree, treeback, qn, dqn, total, parts, arrived,
-    fpad, fone, ftwo, fsend, fy, zsend, zrecv, hsend, hrecv, kvraw,
+    fpad, fone, ftwo, fsend, fy, flow, fmid, flo, flsend, usend, urecv, last, zsend, zrecv,
+    kvraw,
     send_sem, recv_sem, local_sem,
 ):
     s = lax.axis_index("seq")
@@ -97,106 +98,107 @@
         return remote(dst, dst, sem, across)
 
     HX = 0
-    AZ = 1
-    BZ = AZ + 16
-    AY = BZ + 16
-    BY = AY + 64
-    KV = BY + 4
+    AZ = HX + 1
+    BZ = AZ + 32
+    AY = BZ + 32
+    BY = AY + 96
+    BX = BY + 4
+    KV = BX + 16
     DK = KV + 8
-    GR = DK + 8
+    GR = DK + 16
     FY = GR + 3
-    FZ = FY + 6
-    FH = FZ + 16
-
-    def rows(lo, n):
-        return pl.ds(lo, n)
-
-    def a_piece(zz, yy, lo, n):
-        return full.at[:, zz, yy, rows(lo, n), :]
-
-    def b_piece(zz, lo, n):
-        return full.at[:, zz, :, rows(lo, n), :]
-
-    def az(k, side, last=False):
-        zz = zi(-(k - 1)) if side == 0 else zi(k - 1)
-        ref = a_piece(zz, y, 16 * side if last else 0, 16 if last else 32)
-        return remote(ref, ref, AZ + 2 * (k - 1) + side, at_z(1 if side == 0 else -1))
-
-    def az_in(k, side, last=False):
-        zz = zi(-k) if side == 0 else zi(k)
-        ref = a_piece(zz, y, 16 * side if last else 0, 16 if last else 32)
-        return here(ref, AZ + 2 * (k - 1) + side)
-
-    def bz(k, side, last=False):
-        zz = zi(-(k - 1)) if side == 0 else zi(k - 1)
-        ref = b_piece(zz, 32 + 16 * side if last else 32, 16 if last else 32)
-        return remote(ref, ref, BZ + 2 * (k - 1) + side, at_z(1 if side == 0 else -1))
-
-    def bz_in(k, side, last=False):
-        zz = zi(-k) if side == 0 else zi(k)
-        ref = b_piece(zz, 32 + 16 * side if last else 32, 16 if last else 32)
-        return here(ref, BZ + 2 * (k - 1) + side)
-
-    def ring_y(zz, sem, lo):
-        own = a_piece(zz, y, lo, 32)
-        first = [
-            remote(own, own, sem, at_y(1)),
-            remote(own, own, sem + 1, at_y(3)),
-        ]
-        left, right, far = yi(3), yi(1), yi(2)
-        first_in = [
-            here(a_piece(zz, left, lo, 32), sem),
-            here(a_piece(zz, right, lo, 32), sem + 1),
-        ]
-        up = a_piece(zz, left, lo, 16)
-        down = a_piece(zz, right, lo + 16, 16)
-        second = [
-            remote(up, up, sem + 2, at_y(1)),
-            remote(down, down, sem + 3, at_y(3)),
-        ]
-        second_in = [
-            here(a_piece(zz, far, lo, 16), sem + 2),
-            here(a_piece(zz, far, lo + 16, 16), sem + 3),
-        ]
-        return first, first_in, second, second_in
-
-    def ay(step, index):
-        return ring_y(zi(step), AY + 4 * index, 0)
-
-    def ay_start(step, index):
-        for copy in ay(step, index)[0]:
-            copy.start()
-
-    def ay_forward(step, index):
-        first, first_in, second, second_in = ay(step, index)
-        for side in range(2):
-            first_in[side].wait_recv()
-            second[side].start()
-
-    def ay_finish(step, index):
-        first, first_in, second, second_in = ay(step, index)
-        for side in range(2):
-            second_in[side].wait_recv()
-            first[side].wait_send()
-            second[side].wait_send()
+    FL = FY + 6
+    FH = FL + 6
+    FZ = FH + 2
+
+    side_z = lambda side: at_z(1 if side == 0 else -1)
+    xs = (h, 1 - h)
+
+    def a_piece(c, zz, yy):
+        return full.at[xs[c], zz, yy, pl.ds(0, 32), :]
+
+    def b_piece(zz, b):
+        return full.at[h, zz, :, pl.ds(32 + 16 * b, 16), :]
+
+    def az(c, k, side):
+        ref = a_piece(c, zi(1 - k) if side == 0 else zi(k - 1), y)
+        return remote(ref, ref, AZ + 16 * c + 2 * (k - 1) + side, side_z(side))
+
+    def az_in(c, k, side):
+        ref = a_piece(c, zi(-k) if side == 0 else zi(k), y)
+        return here(ref, AZ + 16 * c + 2 * (k - 1) + side)
+
+    def bz(b, k, side):
+        ref = b_piece(zi(1 - k) if side == 0 else zi(k - 1), b)
+        return remote(ref, ref, BZ + 16 * b + 2 * (k - 1) + side, side_z(side))
+
+    def bz_in(b, k, side):
+        ref = b_piece(zi(-k) if side == 0 else zi(k), b)
+        return here(ref, BZ + 16 * b + 2 * (k - 1) + side)
+
+    def bx(step, index):
+        ref = full.at[h, zi(step), :, pl.ds(32, 32), :]
+        return remote(ref, ref, BX + index, across)
+
+    def bx_in(step, index):
+        return here(full.at[1 - h, zi(step), :, pl.ds(32, 32), :], BX + index)
+
+    left, right, far = yi(3), yi(1), yi(2)
+
+    def ay_start(c, step, index):
+        sem = AY + 48 * c + 3 * index
+        own = a_piece(c, zi(step), y)
+        remote(own, own, sem, at_y(1)).start()
+        remote(own, own, sem + 1, at_y(3)).start()
+
+    def ay_forward(c, step, index):
+        sem = AY + 48 * c + 3 * index
+        zz = zi(step)
+        here(a_piece(c, zz, left), sem).wait_recv()
+        here(a_piece(c, zz, right), sem + 1).wait_recv()
+        ref = a_piece(c, zz, right if c else left)
+        remote(ref, ref, sem + 2, at_y(3 if c else 1)).start()
+
+    def ay_finish(c, step, index):
+        sem = AY + 48 * c + 3 * index
+        zz = zi(step)
+        here(a_piece(c, zz, far), sem + 2).wait_recv()
+        own = a_piece(c, zz, y)
+        for i in range(3):
+            here(own, sem + i).wait_send()
 
     own_slot = full.at[h, z, y]
-    cross = remote(piece, own_slot, HX, across)
+    cross = remote(piece.at[pl.ds(0, 32)], own_slot.at[pl.ds(0, 32)], HX, across)
     cross.start()
     keep = pltpu.make_async_copy(piece, own_slot, local_sem.at[0])
     keep.start()
     keep.wait()
-    here(full.at[1 - h, z, y], HX).wait_recv()
-
-    b_first, b_first_in, b_second, b_second_in = ring_y(z, BY, 32)
+
+    def by_piece(yy, lo, n):
+        return full.at[h, z, yy, pl.ds(lo, n), :]
+
+    mine = by_piece(y, 32, 32)
+    by_first = [remote(mine, mine, BY, at_y(1)), remote(mine, mine, BY + 1, at_y(3))]
+    for copy in by_first:
+        copy.start()
     for side in range(2):
-        b_first[side].start()
+        az(0, 1, side).start()
+    ay_start(0, 0, 0)
+    here(a_piece(1, z, y), HX).wait_recv()
     for side in range(2):
-        az(1, side).start()
-    ay_start(0, 0)
-    for side in range(2):
-        b_first_in[side].wait_recv()
-        b_second[side].start()
+        az(1, 1, side).start()
+    ay_start(1, 0, 0)
+    up, down = by_piece(left, 32, 16), by_piece(right, 48, 16)
+    by_second = [remote(up, up, BY + 2, at_y(1)), remote(down, down, BY + 3, at_y(3))]
+    here(by_piece(left, 32, 32), BY).wait_recv()
+    by_second[0].start()
+    here(by_piece(right, 32, 32), BY + 1).wait_recv()
+    by_second[1].start()
+    for i in range(2):
+        here(by_piece(far, 32 + 16 * i, 16), BY + 2 + i).wait_recv()
+        for side in range(2):
+            bz(i, 1, side).start()
+    bx(0, 0).start()
 
     def selection(j):
         first_row = SPAN * j
@@ -215,65 +217,80 @@
         spread = dot(g_ref[:, pl.ds(low, WIN)], select)
         lhs[j, 2 * TOK :] = pltpu.roll(spread, 2 * ROWS, 1).astype(BF16)
 
+    def place_of(k, side):
+        return (-k if side == 0 else k), 2 * k - 1 + side
+
+    def step_of(k, final):
+        for c in range(2):
+            for side in range(2):
+                az_in(c, k, side).wait_recv()
+                if not final or side == c:
+                    az(c, k + 1, side).start()
+                ay_start(c, *place_of(k, side))
+        for b in range(2):
+            for side in range(2):
+                bz_in(b, k, side).wait_recv()
+                if not final or side == b:
+                    bz(b, k + 1, side).start()
+        for side in range(2):
+            bx(*place_of(k, side)).start()
+
+    def forward_of(k):
+        for c in range(2):
+            for side in range(2):
+                ay_forward(c, *place_of(k, side))
+
     prepare(0)
-    for side in range(2):
-        b_second_in[side].wait_recv()
-    for side in range(2):
-        bz(1, side).start()
-
-    def step_of(k, last_z, last_next):
-        for side in range(2):
-            az_in(k, side, last_z).wait_recv()
-            if not last_z:
-                az(k + 1, side, last_next).start()
-        if last_z:
-            ay_start(8, 15)
-        else:
-            ay_start(-k, 2 * k - 1)
-            ay_start(k, 2 * k)
-        for side in range(2):
-            bz_in(k, side, last_z).wait_recv()
-            if not last_z:
-                bz(k + 1, side, last_next).start()
-
-    step_of(1, False, False)
-    ay_forward(0, 0)
+    step_of(1, False)
+    for c in range(2):
+        ay_forward(c, 0, 0)
     prepare(1)
 
     def steps(k, carry):
-        step_of(k, False, False)
-        ay_forward(1 - k, 2 * k - 3)
-        ay_forward(k - 1, 2 * k - 2)
+        step_of(k, False)
+        forward_of(k - 1)
         prepare(k)
         return carry
 
     lax.fori_loop(2, 7, steps, 0)
-    step_of(7, False, True)
-    ay_forward(-6, 11)
-    ay_forward(6, 12)
+    step_of(7, True)
+    forward_of(6)
     prepare(7)
-    step_of(8, True, True)
-    ay_forward(-7, 13)
-    ay_forward(7, 14)
-    ay_forward(8, 15)
+    for c in range(2):
+        az_in(c, 8, c).wait_recv()
+        ay_start(c, 8, 15)
+    for b in range(2):
+        bz_in(b, 8, b).wait_recv()
+    bx(8, 15).start()
+    forward_of(7)
+    for c in range(2):
+        ay_forward(c, 8, 15)
 
     cross.wait_send()
-    for side in range(2):
-        b_first[side].wait_send()
-        b_second[side].wait_send()
-    for k in range(1, 9):
+    for copy in by_first + by_second:
+        copy.wait_send()
+    for c in range(2):
+        ay_finish(c, 0, 0)
+    bx_in(0, 0).wait_recv()
+    bx(0, 0).wait_send()
+
+    def finish(k, carry):
         for side in range(2):
-            az(k, side, k == 8).wait_send()
-            bz(k, side, k == 8).wait_send()
-    ay_finish(0, 0)
-
-    def finish(k, carry):
-        ay_finish(-k, 2 * k - 1)
-        ay_finish(k, 2 * k)
+            for c in range(2):
+                az(c, k, side).wait_send()
+                bz(c, k, side).wait_send()
+                ay_finish(c, *place_of(k, side))
+            bx_in(*place_of(k, side)).wait_recv()
+            bx(*place_of(k, side)).wait_send()
         return carry
 
     lax.fori_loop(1, 8, finish, 0)
-    ay_finish(8, 15)
+    for c in range(2):
+        az(c, 8, c).wait_send()
+        bz(c, 8, c).wait_send()
+        ay_finish(c, 8, 15)
+    bx_in(8, 15).wait_recv()
+    bx(8, 15).wait_send()
 
     def weights(j):
         return full[j // 4, pl.ds(4 * lax.rem(j, 4), 4)].reshape(GROUP * SLOT, 512)
@@ -299,9 +316,8 @@
         ).astype(BF16)
 
     hop4 = remote(ctx.at[0], ctx.at[4], KV, shifted(4))
-    hop8 = remote(ctx.at[0], ctx.at[8], KV + 1, shifted(8))
+    hop8 = remote(ctx.at[4], ctx.at[8], KV + 1, shifted(4))
     hop4.start()
-    hop8.start()
 
     def side_copies(e):
         low = jnp.where(y + e < NY, 0, 4)
@@ -317,6 +333,7 @@
         cols = slice(i * 128, (i + 1) * 128)
         dqn[i // 2, (i % 2) * TOK : (i % 2 + 1) * TOK] = acc[2 * TOK :, cols].astype(BF16)
     here(ctx.at[4], KV).wait_recv()
+    hop8.start()
     for e in range(1, NY):
         @pl.when(y + e < NY)
         def _():
@@ -370,13 +387,51 @@
                 dquery[r * TOK : (r + 1) * TOK], acc[TOK : 2 * TOK, col], q_gain, cosine, sine
             ).astype(BF16)
 
-    for e in range(1, NY):
-        remote(dctx.at[e], ret.at[e - 1, 0], DK + 2 * e, at_y(NY - e)).start()
-        remote(dctx.at[e + 4], ret.at[e - 1, 1], DK + 2 * e + 1, at_y(NY - e)).start()
+    def side_back(e, which):
+        sem = DK + 6 * which + 2 * (e - 1)
+        return [
+            remote(dctx.at[e + 4 * i, which], ret.at[e - 1, i, which], sem + i, at_y(NY - e))
+            for i in range(2)
+        ]
+
+    def tree_back(which):
+        sem = DK + 12 + 2 * which
+        return [
+            remote(tree.at[which, i], treeback.at[which, i], sem + i, shifted(-4 * (i + 1)))
+            for i in range(2)
+        ]
+
+    for which in (1, 0):
+        for e in range(1, NY):
+            for copy in side_back(e, which):
+                copy.start()
+
+    def gather_sums(which):
+        sums = [dctx[4 * i, which].astype(F32) for i in range(3)]
+        for e in range(1, NY):
+            for i in range(2):
+                here(ret.at[e - 1, i, which], DK + 6 * which + 2 * (e - 1) + i).wait_recv()
+            same = y + e < NY
+            one = ret[e - 1, 0, which].astype(F32)
+            two = ret[e - 1, 1, which].astype(F32)
+            sums[0] += jnp.where(same, one, 0.0)
+            sums[1] += jnp.where(same, two, one)
+            sums[2] += jnp.where(same, 0.0, two)
+        tree[which, 0] = sums[1].astype(BF16)
+        tree[which, 1] = sums[2].astype(BF16)
+        for copy in tree_back(which):
+            copy.start()
+        return sums[0]
+
+    def whole(which, own):
+        for i in range(2):
+            here(treeback.at[which, i], DK + 12 + 2 * which + i).wait_recv()
+            own = own + treeback[which, i].astype(F32)
+        return own
 
     total[...] = jnp.zeros_like(total)
 
-    def spread_back(which):
+    def spread_back(which, lo, hi):
         low_slot = ROWS if which == 0 else 0
 
         def run(j, carry):
@@ -391,35 +446,12 @@
             total[:, pl.ds(low, WIN)] += dot(out, select)
             return carry
 
-        lax.fori_loop(0, SEQ // GROUP, run, 0)
-
-    sums = [dctx[4 * i].astype(F32) for i in range(3)]
-    for e in range(1, NY):
-        here(ret.at[e - 1, 0], DK + 2 * e).wait_recv()
-        here(ret.at[e - 1, 1], DK + 2 * e + 1).wait_recv()
-        same = y + e < NY
-        one = ret[e - 1, 0].astype(F32)
-        two = ret[e - 1, 1].astype(F32)
-        sums[0] += jnp.where(same, one, 0.0)
-        sums[1] += jnp.where(same, two, one)
-        sums[2] += jnp.where(same, 0.0, two)
-    tree[0] = sums[1].astype(BF16)
-    tree[1] = sums[2].astype(BF16)
-    back4 = remote(tree.at[0], treeback.at[0], DK, shifted(-4))
-    back8 = remote(tree.at[1], treeback.at[1], DK + 1, shifted(-8))
-    back4.start()
-    back8.start()
-    kvown = sums[0]
-    spread_back(0)
-    here(treeback.at[0], DK).wait_recv()
-    here(treeback.at[1], DK + 1).wait_recv()
-    kvgrad = kvown + treeback[0].astype(F32) + treeback[1].astype(F32)
-    back4.wait_send()
-    back8.wait_send()
-    for e in range(1, NY):
-        remote(dctx.at[e], ret.at[e - 1, 0], DK + 2 * e, at_y(NY - e)).wait_send()
-        remote(dctx.at[e + 4], ret.at[e - 1, 1], DK + 2 * e + 1, at_y(NY - e)).wait_send()
-    dvalue = kvgrad[1]
+        lax.fori_loop(lo, hi, run, 0)
+
+    spread_back(0, 0, 4)
+    own_dv = gather_sums(1)
+    own_dk = gather_sums(0)
+    dvalue = whole(1, own_dv)
 
     place = iota((FSLOT, SPAN), 1)
     slot = iota((FSLOT, SPAN), 0)
@@ -448,31 +480,77 @@
 
     lax.fori_loop(0, SEQ // GROUP, slots, 0)
 
-    far, right, left = yi(2), yi(1), yi(3)
-    f1 = remote(fpad.at[0, :, far], ftwo.at[0], FY, at_y(1))
-    f2 = remote(fpad.at[1, :, far], ftwo.at[1], FY + 1, at_y(3))
-    f3 = remote(fpad.at[1, :, right], ftwo.at[2], FY + 2, at_y(1))
-    f4 = remote(fpad.at[0, :, left], ftwo.at[3], FY + 3, at_y(3))
-    for copy in (f1, f2, f3, f4):
+    cross_low = remote(fpad.at[1 - h, pl.ds(0, 8)], flow, FH, across)
+    cross_low.start()
+
+    def ring(pick, buf, sem):
+        return [
+            remote(pick(0, far), buf.at[0], sem, at_y(1)),
+            remote(pick(1, far), buf.at[1], sem + 1, at_y(3)),
+            remote(pick(1, right), buf.at[2], sem + 2, at_y(1)),
+            remote(pick(0, left), buf.at[3], sem + 3, at_y(3)),
+        ]
+
+    def ring_next(pick_value, buf, send, sem):
+        here(buf.at[0], sem).wait_recv()
+        send[0] = (pick_value(0, right) + buf[0].astype(F32)).astype(BF16)
+        one = remote(send.at[0], buf.at[4], sem + 4, at_y(1))
+        one.start()
+        here(buf.at[1], sem + 1).wait_recv()
+        send[1] = (pick_value(1, left) + buf[1].astype(F32)).astype(BF16)
+        two = remote(send.at[1], buf.at[5], sem + 5, at_y(3))
+        two.start()
+        return [one, two]
+
+    def ring_end(pick_value, buf, sem):
+        for i in range(2, 6):
+            here(buf.at[i], sem + i).wait_recv()
+        first = pick_value(0, y) + buf[4].astype(F32) + buf[3].astype(F32)
+        second = pick_value(1, y) + buf[2].astype(F32) + buf[5].astype(F32)
+        return first, second
+
+    up_ring = ring(lambda i, yy: fpad.at[i, pl.ds(8, 8), yy], ftwo, FY)
+    for copy in up_ring:
         copy.start()
-
+    spread_back(0, 4, 8)
+    up_value = lambda i, yy: fpad[i, 8:16, yy].astype(F32)
+    up_ring += ring_next(up_value, ftwo, fsend, FY)
+
+    here(flow, FH).wait_recv()
+    fmid[...] = (fpad[h, 0:8].astype(F32) + flow[...].astype(F32)).astype(BF16)
+    low_ring = ring(lambda i, yy: fmid.at[pl.ds(4 * i, 4), yy], flo, FL)
+    for copy in low_ring:
+        copy.start()
+
+    dkey = whole(0, own_dk)
     for i in range(2):
         cols = slice(i * 128, (i + 1) * 128)
         kvraw[1, :, cols] = norm_backward(
-            kvgrad[0, :, cols], acc[0:TOK, cols], k_gain, cosine, sine
+            dkey[:, cols], acc[0:TOK, cols], k_gain, cosine, sine
         ).astype(BF16)
     kvraw[1, :, 256:512] = dvalue.astype(BF16)
-
-    here(ftwo.at[0], FY).wait_recv()
-    fsend[0] = (fpad[0, :, right].astype(F32) + ftwo[0].astype(F32)).astype(BF16)
-    f5 = remote(fsend.at[0], ftwo.at[4], FY + 4, at_y(1))
-    f5.start()
-    here(ftwo.at[1], FY + 1).wait_recv()
-    fsend[1] = (fpad[1, :, left].astype(F32) + ftwo[1].astype(F32)).astype(BF16)
-    f6 = remote(fsend.at[1], ftwo.at[5], FY + 5, at_y(3))
-    f6.start()
-
-    spread_back(1)
+    spread_back(1, 0, 2)
+
+    fy[0], fy[1] = ring_end(up_value, ftwo, FY)
+    usend[...] = fy[1 - h].astype(BF16)
+    cross_up = remote(usend, urecv, FH + 1, across)
+    cross_up.start()
+    low_value = lambda i, yy: fmid[4 * i : 4 * i + 4, yy].astype(F32)
+    low_ring += ring_next(low_value, flo, flsend, FL)
+
+    spread_back(1, 2, 5)
+    last[0:4], last[4:8] = ring_end(low_value, flo, FL)
+    here(urecv, FH + 1).wait_recv()
+    last[8:16] = fy[h] + urecv[...].astype(F32)
+    zsend[...] = last[...].astype(BF16)
+
+    def to_z(d):
+        return remote(zsend.at[zi(d)], zrecv.at[d - 1], FZ + d - 1, at_z(d))
+
+    for d in (8, 7, 9, 6, 10, 5, 11, 4, 12, 3, 13, 2, 14, 1, 15):
+        to_z(d).start()
+
+    spread_back(1, 5, 8)
     for i in range(NHEAD):
         parts[i] = total[i * 32 : (i + 1) * 32].astype(BF16)
     shares = []
@@ -481,43 +559,11 @@
         shares.append(remote(parts.at[to], arrived.at[e - 1], GR + e - 1, to, "head"))
         shares[-1].start()
 
-    for i in range(2, 6):
-        here(ftwo.at[i], FY + i).wait_recv()
-    fy[0] = fpad[0, :, y].astype(F32) + ftwo[4].astype(F32) + ftwo[3].astype(F32)
-    fy[1] = fpad[1, :, y].astype(F32) + ftwo[2].astype(F32) + ftwo[5].astype(F32)
-
-    def fz(k, side, first=False):
-        i = 2 * (k - 1) + side
-        src, dst = zsend.at[i], zrecv.at[i]
-        if first:
-            src, dst = src.at[side], dst.at[side]
-        return remote(src, dst, FZ + i, at_z(1 if side == 0 else -1))
-
-    def fz_in(k, side, first=False):
-        i = 2 * (k - 1) + side
-        return here(zrecv.at[i].at[side] if first else zrecv.at[i], FZ + i)
-
-    for side in range(2):
-        zsend[side, side] = fy[side, zi(8)].astype(BF16)
-        fz(1, side, True).start()
-    for k in range(1, 8):
-        for side in range(2):
-            fz_in(k, side, k == 1).wait_recv()
-            i = 2 * (k - 1) + side
-            own = zi(8 - k) if side == 0 else zi(k - 8)
-            for part in range(2):
-                value = fy[part, own]
-                if k > 1 or part == side:
-                    value = value + zrecv[i, part].astype(F32)
-                zsend[i + 2, part] = value.astype(BF16)
-            fz(k + 1, side).start()
-    for side in range(2):
-        fz_in(8, side).wait_recv()
-    sums = [fy[p, z] + zrecv[14, p].astype(F32) + zrecv[15, p].astype(F32) for p in range(2)]
-    low_half = h == 0
-    hsend[...] = jnp.where(low_half, sums[1], sums[0]).astype(BF16)
-    last = remote(hsend, hrecv, FH, across)
-    last.start()
+    sums = last[z]
+    for d in range(1, NZ):
+        here(zrecv.at[d - 1], FZ + d - 1).wait_recv()
+        sums = sums + zrecv[d - 1].astype(F32)
+    fv_ref[...] = sums * (1.0 / (SEQ * TOK))
 
     for e in range(1, NHEAD):
         here(arrived.at[e - 1], GR + e - 1).wait_recv()
@@ -525,24 +571,22 @@
     for e in range(1, NHEAD):
         mine = mine + arrived[e - 1].astype(F32)
     gi_ref[...] = mine.astype(BF16)
-    for copy in shares:
+
+    for copy in shares + up_ring + low_ring + [cross_low, cross_up]:
         copy.wait_send()
-
-    here(hrecv, FH).wait_recv()
-    fv_ref[...] = (jnp.where(low_half, sums[0], sums[1]) + hrecv[...].astype(F32)) * (
-        1.0 / (SEQ * TOK)
-    )
-    last.wait_send()
-    for copy in (f1, f2, f3, f4, f5, f6):
-        copy.wait_send()
-    for k in range(1, 9):
-        for side in range(2):
-            fz(k, side, k == 1).wait_send()
+    for d in range(1, NZ):
+        to_z(d).wait_send()
+    for which in range(2):
+        for copy in tree_back(which):
+            copy.wait_send()
+        for e in range(1, NY):
+            for copy in side_back(e, which):
+                copy.wait_send()
 
 
 def layer(piece, x, g, starts, cosine, sine, q_gain, k_gain):
     vmem = pl.BlockSpec(memory_space=pltpu.VMEM)
-    sems = 160
+    sems = 256
     return pl.pallas_call(
         body,
         name="layer_backward",
@@ -568,13 +612,18 @@
             pltpu.VMEM((NHEAD - 1, 32, WIDTH), BF16),
             pltpu.VMEM((NH, NZ, NY, FSLOT, 128), BF16),
             pltpu.VMEM((WIDTH, 256), BF16),
-            pltpu.VMEM((6, NZ, FSLOT, 128), BF16),
-            pltpu.VMEM((2, NZ, FSLOT, 128), BF16),
-            pltpu.VMEM((NH, NZ, FSLOT, 128), F32),
-            pltpu.VMEM((16, NH, FSLOT, 128), BF16),
-            pltpu.VMEM((16, NH, FSLOT, 128), BF16),
-            pltpu.VMEM((FSLOT, 128), BF16),
-            pltpu.VMEM((FSLOT, 128), BF16),
+            pltpu.VMEM((6, 8, FSLOT, 128), BF16),
+            pltpu.VMEM((2, 8, FSLOT, 128), BF16),
+            pltpu.VMEM((NH, 8, FSLOT, 128), F32),
+            pltpu.VMEM((8, NY, FSLOT, 128), BF16),
+            pltpu.VMEM((8, NY, FSLOT, 128), BF16),
+            pltpu.VMEM((6, 4, FSLOT, 128), BF16),
+            pltpu.VMEM((2, 4, FSLOT, 128), BF16),
+            pltpu.VMEM((8, FSLOT, 128), BF16),
+            pltpu.VMEM((8, FSLOT, 128), BF16),
+            pltpu.VMEM((NZ, FSLOT, 128), F32),
+            pltpu.VMEM((NZ, FSLOT, 128), BF16),
+            pltpu.VMEM((NZ - 1, FSLOT, 128), BF16),
             pltpu.VMEM((2, TOK, 512), BF16),
             pltpu.SemaphoreType.DMA((sems,)),
             pltpu.SemaphoreType.DMA((sems,)),

time: 190 us -> 152 us (0.80); the launches traced: 190 us -> 149 us
  Pallas kernels: 181 us -> 141 us
    pallas_call x1, Pallas kernels: 181 us -> 141 us  [layer(): pl.pallas_call(body, name='layer_backward', out_shape=(jax.ShapeDtypeStru...]
where the time goes in v2:
time: 152 us; the launch traced here: 149 us
  Pallas kernels  141 us (93%)
  other arithmetic  5.11 us (3%)
  local copies, waits for them, and re-layouts  2.48 us (2%)
    pallas_call x1, Pallas kernels, layer(): pl.pallas_call(body, name='layer_backward', out_shape=(jax.ShapeDtypeStru...  141 us

profile of v2, /device:TPU:6, one launch (start us, length us, event | category | flops | bytes accessed | tf_op | source)
XLA Modules:
  0.0 149.2 jit_solution(16111681329185556415)
XLA Ops:
  0.6 0.0 copy-start
  0.6 0.7 subtract_convert_fusion
  1.3 0.1 pad.12.clone
  1.4 1.3 pad_add_fusion
  2.7 0.0 copy-done
  2.7 1.4 maximum_maximum_fusion.piece
  4.1 0.3 fusion
  4.5 0.8 pad_maximum_fusion
  5.2 140.9 %layer_backward.1 = (bf16[32,2688]{1,0:T(8,128)(2,1)}, f32[48,128]{1,0:T(8,128)}) custom-call(bf16[64,512]{1,0:T(8,128)(2,1)} %maximum_maximum_fusion.piece, bf16[128,2688]{1,0:T(8,128)(2,1)} %x_ref.1, bf16[128,2688]{1,0:T(8,128)(2,1)} %g_ref.1, s32[1,256]{1,0:T(1,128)} %bitcast.6, f32[128,128]{1,0:T(8,128)} %get-tuple-element.11.cos_ref, ...), custom_call_target="tpu_custom_call" | custom-call | tf_op jit(solution)/shard_map/layer_backward/pallas_call | solution.py:590
  146.2 0.8 fusion.1
  147.0 0.6 pad_maximum_fusion.2
  147.6 1.6 %copy.12 = bf16[32,2688]{1,0:T(8,128)(2,1)} copy(bf16[32,2688]{1,0:T(8,128)(2,1)} %get-tuple-element.16) | data formatting | bytes 344064
  (1 shorter events, 0.0 us)
Async XLA Ops:
  0.6 2.1 %copy-start = (bf16[512,21]{0,1:T(8,128)(2,1)S(1)}, bf16[512,21]{0,1:T(8,128)(2,1)}, u32[]{:S(2)}) copy-start(bf16[512,21]{0,1:T(8,128)(2,1)} %param.15) | copy-start | bytes 64516

commit v3 on v2

--- a/solution.py
+++ b/solution.py
@@ -20,6 +20,7 @@
 GROUP = 16
 SPAN = GROUP * ROWS
 WIN = 512
+EDGE = 384
 F32 = jnp.float32
 BF16 = jnp.bfloat16
 
@@ -49,10 +50,10 @@
 
 
 def body(
-    piece, x_ref, g_ref, start_ref, cos_ref, sin_ref, qg_ref, kg_ref,
+    x_hbm, g_hbm, wk_ref, wv_ref, wq_ref, wo_ref, start_ref, cos_ref, sin_ref, qg_ref, kg_ref,
     gi_ref, fv_ref,
-    full, lhs, acc, ctx, dctx, ret, tree, treeback, qn, dqn, total, parts, arrived,
-    fpad, fone, ftwo, fsend, fy, flow, fmid, flo, flsend, usend, urecv, last, zsend, zrecv,
+    x_ref, g_ref, squares, full, lhs, acc, ctx, dctx, ret, tree, treeback, qn, dqn, total, parts, arrived,
+    fpad, ftwo, fsend, fy, flow, fmid, flo, flsend, usend, urecv, last, zsend, zrecv,
     kvraw,
     send_sem, recv_sem, local_sem,
 ):
@@ -83,6 +84,20 @@
         pl.semaphore_signal(barrier, inc=1, device_id={"seq": partner})
     for e in range(1, NHEAD):
         pl.semaphore_signal(barrier, inc=1, device_id={"head": lax.rem(hd + e, NHEAD)})
+    load_x = pltpu.make_async_copy(x_hbm, x_ref, local_sem.at[0])
+    load_g = pltpu.make_async_copy(g_hbm, g_ref, local_sem.at[1])
+    load_x.start()
+    load_g.start()
+
+    def rows_at(first):
+        return jnp.where(
+            iota((SLOT, ROWS), 0) == iota((SLOT, ROWS), 1) + first, 1.0, 0.0
+        ).astype(BF16)
+
+    rest = dot(rows_at(ROWS), wq_ref[...]) + dot(rows_at(2 * ROWS), wo_ref[...], 1, 1)
+    own_slot = full.at[h, z, y]
+    own_slot[:, 0:256] = (dot(rows_at(0), wk_ref[...]) + rest[:, 0:256]).astype(BF16)
+    own_slot[:, 256:512] = (dot(rows_at(0), wv_ref[...]) + rest[:, 256:512]).astype(BF16)
     pl.semaphore_wait(barrier, len(seq_partners) + NHEAD - 1)
 
     def remote(src, dst, sem, target, axis="seq"):
@@ -110,6 +125,9 @@
     FL = FY + 6
     FH = FL + 6
     FZ = FH + 2
+    HY = FZ + 15
+    CY = HY + 1
+    CZ = CY + 4
 
     side_z = lambda side: at_z(1 if side == 0 else -1)
     xs = (h, 1 - h)
@@ -137,11 +155,21 @@
         return here(ref, BZ + 16 * b + 2 * (k - 1) + side)
 
     def bx(step, index):
-        ref = full.at[h, zi(step), :, pl.ds(32, 32), :]
+        ref = full.at[h, zi(step), :, pl.ds(32, 32), pl.ds(0, EDGE)]
         return remote(ref, ref, BX + index, across)
 
     def bx_in(step, index):
-        return here(full.at[1 - h, zi(step), :, pl.ds(32, 32), :], BX + index)
+        return here(full.at[1 - h, zi(step), :, pl.ds(32, 32), pl.ds(0, EDGE)], BX + index)
+
+    def c_piece(zz):
+        return full.at[1 - h, zz, :, pl.ds(32, 32), pl.ds(EDGE, 512 - EDGE)]
+
+    def cz(k, side):
+        ref = c_piece(zi(1 - k) if side == 0 else zi(k - 1))
+        return remote(ref, ref, CZ + 2 * (k - 1) + side, side_z(side))
+
+    def cz_in(k, side):
+        return here(c_piece(zi(-k) if side == 0 else zi(k)), CZ + 2 * (k - 1) + side)
 
     left, right, far = yi(3), yi(1), yi(2)
 
@@ -167,12 +195,15 @@
         for i in range(3):
             here(own, sem + i).wait_send()
 
-    own_slot = full.at[h, z, y]
-    cross = remote(piece.at[pl.ds(0, 32)], own_slot.at[pl.ds(0, 32)], HX, across)
-    cross.start()
-    keep = pltpu.make_async_copy(piece, own_slot, local_sem.at[0])
-    keep.start()
-    keep.wait()
+    def hx_piece(hh, lo, first):
+        return full.at[hh, z, y, pl.ds(lo, 32), pl.ds(first, 512 - first)]
+
+    cross = [
+        remote(hx_piece(h, lo, first), hx_piece(h, lo, first), sem, across)
+        for lo, first, sem in ((0, 0, HX), (32, EDGE, HY))
+    ]
+    for copy in cross:
+        copy.start()
 
     def by_piece(yy, lo, n):
         return full.at[h, z, yy, pl.ds(lo, n), :]
@@ -188,6 +219,15 @@
     for side in range(2):
         az(1, 1, side).start()
     ay_start(1, 0, 0)
+    here(hx_piece(1 - h, 32, EDGE), HY).wait_recv()
+
+    def cy_piece(yy, lo, n):
+        return full.at[1 - h, z, yy, pl.ds(lo, n), pl.ds(EDGE, 512 - EDGE)]
+
+    mine = cy_piece(y, 32, 32)
+    cy_first = [remote(mine, mine, CY, at_y(1)), remote(mine, mine, CY + 1, at_y(3))]
+    for copy in cy_first:
+        copy.start()
     up, down = by_piece(left, 32, 16), by_piece(right, 48, 16)
     by_second = [remote(up, up, BY + 2, at_y(1)), remote(down, down, BY + 3, at_y(3))]
     here(by_piece(left, 32, 32), BY).wait_recv()
@@ -199,6 +239,18 @@
         for side in range(2):
             bz(i, 1, side).start()
     bx(0, 0).start()
+    up, down = cy_piece(left, 32, 16), cy_piece(right, 48, 16)
+    cy_second = [remote(up, up, CY + 2, at_y(1)), remote(down, down, CY + 3, at_y(3))]
+    here(cy_piece(left, 32, 32), CY).wait_recv()
+    cy_second[0].start()
+    here(cy_piece(right, 32, 32), CY + 1).wait_recv()
+    cy_second[1].start()
+    for i in range(2):
+        here(cy_piece(far, 32 + 16 * i, 16), CY + 2 + i).wait_recv()
+    for side in range(2):
+        cz(1, side).start()
+    load_x.wait()
+    load_g.wait()
 
     def selection(j):
         first_row = SPAN * j
@@ -216,6 +268,14 @@
         lhs[j, TOK : 2 * TOK] = pltpu.roll(spread, ROWS, 1).astype(BF16)
         spread = dot(g_ref[:, pl.ds(low, WIN)], select)
         lhs[j, 2 * TOK :] = pltpu.roll(spread, 2 * ROWS, 1).astype(BF16)
+        row = iota((GROUP * FSLOT, 1), 0)
+        owner = (row * 1366) >> 16
+        slot = row - owner * FSLOT
+        slot = jnp.where(slot < ROWS, slot, slot - ROWS)
+        target = jnp.where(slot < ROWS, offset + owner * ROWS + slot, -1)
+        select = jnp.where(iota((GROUP * FSLOT, WIN), 1) == target, 1.0, 0.0).astype(BF16)
+        block = x_ref[:, pl.ds(low, WIN)].astype(F32)
+        squares[j] = dot(select, (block * block).astype(BF16), 1, 1).astype(BF16)
 
     def place_of(k, side):
         return (-k if side == 0 else k), 2 * k - 1 + side
@@ -234,6 +294,10 @@
                     bz(b, k + 1, side).start()
         for side in range(2):
             bx(*place_of(k, side)).start()
+        for side in range(2):
+            cz_in(k, side).wait_recv()
+            if not final or side == 0:
+                cz(k + 1, side).start()
 
     def forward_of(k):
         for c in range(2):
@@ -262,12 +326,12 @@
     for b in range(2):
         bz_in(b, 8, b).wait_recv()
     bx(8, 15).start()
+    cz_in(8, 0).wait_recv()
     forward_of(7)
     for c in range(2):
         ay_forward(c, 8, 15)
 
-    cross.wait_send()
-    for copy in by_first + by_second:
+    for copy in cross + by_first + by_second + cy_first + cy_second:
         copy.wait_send()
     for c in range(2):
         ay_finish(c, 0, 0)
@@ -282,6 +346,7 @@
                 ay_finish(c, *place_of(k, side))
             bx_in(*place_of(k, side)).wait_recv()
             bx(*place_of(k, side)).wait_send()
+            cz(k, side).wait_send()
         return carry
 
     lax.fori_loop(1, 8, finish, 0)
@@ -291,29 +356,27 @@
         ay_finish(c, 8, 15)
     bx_in(8, 15).wait_recv()
     bx(8, 15).wait_send()
+    cz(8, 0).wait_send()
 
     def weights(j):
         return full[j // 4, pl.ds(4 * lax.rem(j, 4), 4)].reshape(GROUP * SLOT, 512)
 
     acc[...] = jnp.zeros_like(acc)
 
-    def project(j, carry):
-        acc[...] += dot(lhs[j], weights(j))
-        return carry
-
-    lax.fori_loop(0, SEQ // GROUP, project, 0)
-
+    def project(lo, hi):
+        def run(j, carry):
+            acc[lo:hi] += dot(lhs[j, lo:hi], weights(j))
+            return carry
+
+        lax.fori_loop(0, SEQ // GROUP, run, 0)
+
+    project(0, TOK)
     cosine, sine = cos_ref[...], sin_ref[...]
     q_gain, k_gain = qg_ref[...], kg_ref[...]
     for i in range(2):
         cols = slice(i * 128, (i + 1) * 128)
         ctx[0, 0, :, cols] = norm_forward(acc[0:TOK, cols], k_gain, cosine, sine).astype(BF16)
     ctx[0, 1] = acc[0:TOK, 256:512].astype(BF16)
-    for i in range(4):
-        cols = slice(i * 128, (i + 1) * 128)
-        qn[i // 2, (i % 2) * TOK : (i % 2 + 1) * TOK] = norm_forward(
-            acc[TOK : 2 * TOK, cols], q_gain, cosine, sine
-        ).astype(BF16)
 
     hop4 = remote(ctx.at[0], ctx.at[4], KV, shifted(4))
     hop8 = remote(ctx.at[4], ctx.at[8], KV + 1, shifted(4))
@@ -329,9 +392,6 @@
         @pl.when(y + e < NY)
         def _():
             side_copies(e)[0].start()
-    for i in range(4):
-        cols = slice(i * 128, (i + 1) * 128)
-        dqn[i // 2, (i % 2) * TOK : (i % 2 + 1) * TOK] = acc[2 * TOK :, cols].astype(BF16)
     here(ctx.at[4], KV).wait_recv()
     hop8.start()
     for e in range(1, NY):
@@ -342,11 +402,19 @@
         @pl.when(y + e >= NY)
         def _():
             side_copies(e)[0].start()
+    project(TOK, 3 * TOK)
     here(ctx.at[8], KV + 1).wait_recv()
     for e in range(1, NY):
         @pl.when(y + e >= NY)
         def _():
             side_copies(e)[1].start()
+    for i in range(4):
+        cols = slice(i * 128, (i + 1) * 128)
+        half = slice((i % 2) * TOK, (i % 2 + 1) * TOK)
+        qn[i // 2, half] = norm_forward(
+            acc[TOK : 2 * TOK, cols], q_gain, cosine, sine
+        ).astype(BF16)
+        dqn[i // 2, half] = acc[2 * TOK :, cols].astype(BF16)
     for e in range(1, NY):
         here(ctx.at[e], KV + 2 * e).wait_recv()
         here(ctx.at[e + 4], KV + 2 * e + 1).wait_recv()
@@ -453,26 +521,11 @@
     own_dk = gather_sums(0)
     dvalue = whole(1, own_dv)
 
-    place = iota((FSLOT, SPAN), 1)
-    slot = iota((FSLOT, SPAN), 0)
-    rank = jnp.where(slot < ROWS, slot, jnp.where(slot < 2 * ROWS, slot - ROWS, -WIDTH))
-    select = jnp.concatenate(
-        [jnp.where(place == rank + ROWS * i, 1.0, 0.0).astype(BF16) for i in range(GROUP)], axis=0
-    )
     first_cols = jnp.where(iota((GROUP, FSLOT, 128), 1) < ROWS, 1.0, 0.0)
     dv_sq = (dvalue * dvalue).astype(BF16)
 
-    def squares(i, carry):
-        block = x_ref[:, pl.ds(pl.multiple_of(i * 384, 128), 384)].astype(F32)
-        fone[pl.ds(pl.multiple_of(i * 384, 128), 384)] = dot(
-            (block * block).astype(BF16), dv_sq, 0, 0
-        ).astype(BF16)
-        return carry
-
-    lax.fori_loop(0, WIDTH // 384, squares, 0)
-
     def slots(j, carry):
-        both = dot(select, fone[pl.ds(pl.multiple_of(SPAN * j, 16), SPAN)])
+        both = dot(squares[j], dv_sq)
         both = both.reshape(GROUP, FSLOT, 256)
         picked = jnp.where(first_cols > 0.5, both[:, :, 0:128], both[:, :, 128:256])
         fpad[j // 4, pl.ds(4 * lax.rem(j, 4), 4)] = picked.astype(BF16).reshape(4, 4, FSLOT, 128)
@@ -563,7 +616,9 @@
     for d in range(1, NZ):
         here(zrecv.at[d - 1], FZ + d - 1).wait_recv()
         sums = sums + zrecv[d - 1].astype(F32)
-    fv_ref[...] = sums * (1.0 / (SEQ * TOK))
+    sums = sums * (1.0 / (SEQ * TOK))
+    fv_ref[:, 0:128] = sums[0:ROWS]
+    fv_ref[:, 128:256] = pltpu.roll(sums, FSLOT - ROWS, 0)[0:ROWS]
 
     for e in range(1, NHEAD):
         here(arrived.at[e - 1], GR + e - 1).wait_recv()
@@ -584,19 +639,22 @@
                 copy.wait_send()
 
 
-def layer(piece, x, g, starts, cosine, sine, q_gain, k_gain):
+def layer(*operands):
     vmem = pl.BlockSpec(memory_space=pltpu.VMEM)
-    sems = 256
+    sems = 320
     return pl.pallas_call(
         body,
         name="layer_backward",
         out_shape=(
             jax.ShapeDtypeStruct((32, WIDTH), BF16),
-            jax.ShapeDtypeStruct((FSLOT, 128), F32),
+            jax.ShapeDtypeStruct((ROWS, 256), F32),
         ),
-        in_specs=[pl.BlockSpec(memory_space=pl.ANY)] + [vmem] * 7,
+        in_specs=[pl.BlockSpec(memory_space=pl.ANY)] * 2 + [vmem] * 9,
         out_specs=(vmem, vmem),
         scratch_shapes=[
+            pltpu.VMEM((TOK, WIDTH), BF16),
+            pltpu.VMEM((TOK, WIDTH), BF16),
+            pltpu.VMEM((SEQ // GROUP, GROUP * FSLOT, TOK), BF16),
             pltpu.VMEM((NH, NZ, NY, SLOT, 512), BF16),
             pltpu.VMEM((SEQ // GROUP, 3 * TOK, GROUP * SLOT), BF16),
             pltpu.VMEM((3 * TOK, 512), F32),
@@ -611,7 +669,6 @@
             pltpu.VMEM((NHEAD, 32, WIDTH), BF16),
             pltpu.VMEM((NHEAD - 1, 32, WIDTH), BF16),
             pltpu.VMEM((NH, NZ, NY, FSLOT, 128), BF16),
-            pltpu.VMEM((WIDTH, 256), BF16),
             pltpu.VMEM((6, 8, FSLOT, 128), BF16),
             pltpu.VMEM((2, 8, FSLOT, 128), BF16),
             pltpu.VMEM((NH, 8, FSLOT, 128), F32),
@@ -627,12 +684,12 @@
             pltpu.VMEM((2, TOK, 512), BF16),
             pltpu.SemaphoreType.DMA((sems,)),
             pltpu.SemaphoreType.DMA((sems,)),
-            pltpu.SemaphoreType.DMA((1,)),
+            pltpu.SemaphoreType.DMA((2,)),
         ],
         compiler_params=pltpu.CompilerParams(
             collective_id=0, has_side_effects=True, vmem_limit_bytes=60 * 1024 * 1024
         ),
-    )(piece, x, g, starts, cosine, sine, q_gain, k_gain)
+    )(*operands)
 
 
 def on_device(
@@ -655,20 +712,11 @@
     cosine, sine = jnp.cos(angles), jnp.sin(angles)
     cosine = jnp.concatenate([cosine, cosine], axis=1)
     sine = jnp.concatenate([-sine, sine], axis=1)
-    piece = jnp.concatenate(
-        [
-            jnp.concatenate([key_weight, value_weight], axis=1),
-            w_query,
-            w_out.T,
-            jnp.zeros((1, 512), BF16),
-        ],
-        axis=0,
+    starts = jnp.concatenate([doc_start, doc_start])[None, :]
+    grad_input, fisher_value = layer(
+        layer_input, grad_out, key_weight, value_weight, w_query, w_out, starts, cosine, sine,
+        q_gain[None, :], key_norm_gain[None, :],
     )
-    starts = jnp.concatenate([doc_start, doc_start])[None, :]
-    grad_input, sums = layer(
-        piece, layer_input, grad_out, starts, cosine, sine, q_gain[None, :], key_norm_gain[None, :]
-    )
-    fisher_value = jnp.concatenate([sums[0:ROWS], sums[ROWS : 2 * ROWS]], axis=1)
     return (fisher_value, grad_input)
 
 

time: 152 us -> 142 us (0.934)
  Pallas kernels: 141 us -> 132 us
  other arithmetic: 5.11 us -> 1.65 us
  local copies, waits for them, and re-layouts: 2.48 us -> 5.11 us
    pallas_call x1, Pallas kernels: 141 us -> 132 us  [layer(): pl.pallas_call(body, name='layer_backward', out_shape=(jax.ShapeDtypeStru...]
    unnamed x3 -> x5, local copies, waits for them, and re-layouts: 1.6 us -> 5.11 us
    concatenate x2 -> x0, other arithmetic: 2.06 us -> none  [the longest x1 1.45 us: on_device(): jnp.concatenate([jnp.concatenate([key_weight, value_weight], axis=1), w_q...]
where the time goes in v3:
time: 142 us; the launch traced here: 139 us
  Pallas kernels  132 us (93%)
  local copies, waits for them, and re-layouts  5.11 us (4%)
  other arithmetic  1.65 us (1%)
    pallas_call x1, Pallas kernels, layer(): pl.pallas_call(body, name='layer_backward', out_shape=(jax.ShapeDtypeStru...  132 us
    unnamed x5, local copies, waits for them, and re-layouts  5.11 us

profile of v3, /device:TPU:6, one launch (start us, length us, event | category | flops | bytes accessed | tf_op | source)
XLA Modules:
  0.0 139.0 jit_solution(16502409613242022286)
XLA Ops:
  0.6 0.0 copy-start
  0.6 0.6 copy-done
  1.3 0.6 pad_add_fusion
  1.9 1.5 %copy.11.wo_ref = bf16[512,21]{1,0:T(8,128)(2,1)} copy(bf16[512,21]{0,1:T(8,128)(2,1)} %param.15) | data formatting | bytes 43008 | tf_op args[6]
  3.4 0.3 fusion
  3.7 0.8 pad_maximum_fusion
  4.5 131.6 %layer_backward.1 = (bf16[32,2688]{1,0:T(8,128)(2,1)}, f32[21,256]{1,0:T(8,128)}) custom-call(bf16[128,2688]{1,0:T(8,128)(2,1)} %x_hbm.1, bf16[128,2688]{1,0:T(8,128)(2,1)} %g_hbm.1, bf16[21,256]{1,0:T(8,128)(2,1)} %wk_ref.1, bf16[21,256]{1,0:T(8,128)(2,1)} %wv_ref.1, bf16[21,512]{1,0:T(8,128)(2,1)} %wq_ref.1, bf16[512,21]{1,0:T(8,128)(2,1)} %copy.11.wo_ref, ...), custom_call_target="tpu_custom_call" | custom-call | tf_op jit(solution)/shard_map/layer_backward/pallas_call | solution.py:645
  136.0 1.3 copy.14
  137.4 1.6 %copy.15 = bf16[32,2688]{1,0:T(8,128)(2,1)} copy(bf16[32,2688]{1,0:T(8,128)(2,1)} %get-tuple-element.14) | data formatting | bytes 344064
  (2 shorter events, 0.0 us)
Async XLA Ops:
  0.6 0.7 copy-start

commit v4 on v3

--- a/solution.py
+++ b/solution.py
@@ -94,7 +94,7 @@
             iota((SLOT, ROWS), 0) == iota((SLOT, ROWS), 1) + first, 1.0, 0.0
         ).astype(BF16)
 
-    rest = dot(rows_at(ROWS), wq_ref[...]) + dot(rows_at(2 * ROWS), wo_ref[...], 1, 1)
+    rest = dot(rows_at(ROWS), wq_ref[...]) + dot(rows_at(2 * ROWS), wo_ref[...])
     own_slot = full.at[h, z, y]
     own_slot[:, 0:256] = (dot(rows_at(0), wk_ref[...]) + rest[:, 0:256]).astype(BF16)
     own_slot[:, 256:512] = (dot(rows_at(0), wv_ref[...]) + rest[:, 256:512]).astype(BF16)
@@ -195,6 +195,17 @@
         for i in range(3):
             here(own, sem + i).wait_send()
 
+    def place_of(k, side):
+        return (-k if side == 0 else k), 2 * k - 1 + side
+
+    def first_step(k, final=False):
+        for c in range(2):
+            for side in range(2):
+                az_in(c, k, side).wait_recv()
+                if not final or side == c:
+                    az(c, k + 1, side).start()
+                ay_start(c, *place_of(k, side))
+
     def hx_piece(hh, lo, first):
         return full.at[hh, z, y, pl.ds(lo, 32), pl.ds(first, 512 - first)]
 
@@ -234,6 +245,7 @@
     by_second[0].start()
     here(by_piece(right, 32, 32), BY + 1).wait_recv()
     by_second[1].start()
+    first_step(1)
     for i in range(2):
         here(by_piece(far, 32 + 16 * i, 16), BY + 2 + i).wait_recv()
         for side in range(2):
@@ -245,12 +257,11 @@
     cy_second[0].start()
     here(cy_piece(right, 32, 32), CY + 1).wait_recv()
     cy_second[1].start()
+    first_step(2)
     for i in range(2):
         here(cy_piece(far, 32 + 16 * i, 16), CY + 2 + i).wait_recv()
     for side in range(2):
         cz(1, side).start()
-    load_x.wait()
-    load_g.wait()
 
     def selection(j):
         first_row = SPAN * j
@@ -277,16 +288,7 @@
         block = x_ref[:, pl.ds(low, WIN)].astype(F32)
         squares[j] = dot(select, (block * block).astype(BF16), 1, 1).astype(BF16)
 
-    def place_of(k, side):
-        return (-k if side == 0 else k), 2 * k - 1 + side
-
-    def step_of(k, final):
-        for c in range(2):
-            for side in range(2):
-                az_in(c, k, side).wait_recv()
-                if not final or side == c:
-                    az(c, k + 1, side).start()
-                ay_start(c, *place_of(k, side))
+    def step_of(k, final=False):
         for b in range(2):
             for side in range(2):
                 bz_in(b, k, side).wait_recv()
@@ -304,32 +306,43 @@
             for side in range(2):
                 ay_forward(c, *place_of(k, side))
 
+    load_x.wait()
+    load_g.wait()
     prepare(0)
-    step_of(1, False)
+    step_of(1)
+    first_step(3)
     for c in range(2):
         ay_forward(c, 0, 0)
-    prepare(1)
+    forward_of(1)
 
     def steps(k, carry):
-        step_of(k, False)
-        forward_of(k - 1)
-        prepare(k)
+        step_of(k)
+        first_step(k + 2)
+        forward_of(k)
+        prepare(k - 1)
         return carry
 
-    lax.fori_loop(2, 7, steps, 0)
-    step_of(7, True)
-    forward_of(6)
-    prepare(7)
+    lax.fori_loop(2, 5, steps, 0)
+    step_of(5)
+    first_step(7, True)
+    forward_of(5)
+    prepare(4)
+    step_of(6)
     for c in range(2):
         az_in(c, 8, c).wait_recv()
         ay_start(c, 8, 15)
+    forward_of(6)
+    prepare(5)
+    step_of(7, True)
+    forward_of(7)
+    prepare(6)
+    for c in range(2):
+        ay_forward(c, 8, 15)
     for b in range(2):
         bz_in(b, 8, b).wait_recv()
     bx(8, 15).start()
     cz_in(8, 0).wait_recv()
-    forward_of(7)
-    for c in range(2):
-        ay_forward(c, 8, 15)
+    prepare(7)
 
     for copy in cross + by_first + by_second + cy_first + cy_second:
         copy.wait_send()
@@ -371,7 +384,8 @@
         lax.fori_loop(0, SEQ // GROUP, run, 0)
 
     project(0, TOK)
-    cosine, sine = cos_ref[...], sin_ref[...]
+    cosine = jnp.concatenate([cos_ref[...], cos_ref[...]], axis=1)
+    sine = jnp.concatenate([-sin_ref[...], sin_ref[...]], axis=1)
     q_gain, k_gain = qg_ref[...], kg_ref[...]
     for i in range(2):
         cols = slice(i * 128, (i + 1) * 128)
@@ -431,7 +445,7 @@
     key_index = s * TOK - (place & ~(TOK - 1)) + (place & (TOK - 1))
     query_index = s * TOK + (iota((1, 2 * TOK), 1) & (TOK - 1))
     visible = (
-        (key_index >= start_ref[...])
+        (key_index >= jnp.concatenate([start_ref[...], start_ref[...]], axis=1))
         & (key_index <= query_index)
         & (query_index - key_index < WINDOW)
     )
@@ -710,11 +724,9 @@
     frequency = jnp.exp(jnp.arange(half).astype(F32) * (-math.log(10000.0) / half))
     angles = positions[:, None] * frequency[None, :]
     cosine, sine = jnp.cos(angles), jnp.sin(angles)
-    cosine = jnp.concatenate([cosine, cosine], axis=1)
-    sine = jnp.concatenate([-sine, sine], axis=1)
-    starts = jnp.concatenate([doc_start, doc_start])[None, :]
     grad_input, fisher_value = layer(
-        layer_input, grad_out, key_weight, value_weight, w_query, w_out, starts, cosine, sine,
+        layer_input, grad_out, key_weight, value_weight, w_query, w_out.T, doc_start[None, :],
+        cosine, sine,
         q_gain[None, :], key_norm_gain[None, :],
     )
     return (fisher_value, grad_input)

time: 142 us -> 138 us (0.972)
  local copies, waits for them, and re-layouts: 5.11 us -> 3.6 us
    unnamed x5 -> x4, local copies, waits for them, and re-layouts: 5.11 us -> 3.6 us
where the time goes in v4:
time: 138 us; the launch traced here: 136 us
  Pallas kernels  131 us (95%)
  local copies, waits for them, and re-layouts  3.6 us (3%)
    pallas_call x1, Pallas kernels, layer(): pl.pallas_call(body, name='layer_backward', out_shape=(jax.ShapeDtypeStru...  131 us
    unnamed x4, local copies, waits for them, and re-layouts  3.6 us

profile of v4, /device:TPU:6, one launch (start us, length us, event | category | flops | bytes accessed | tf_op | source)
XLA Modules:
  0.0 136.2 jit_solution(2071922593100102968)
XLA Ops:
  0.6 0.0 copy-start
  0.6 0.6 copy-done
  1.3 1.0 multiply_sine_fusion
  2.3 131.0 %layer_backward.1 = (bf16[32,2688]{1,0:T(8,128)(2,1)}, f32[21,256]{1,0:T(8,128)}) custom-call(bf16[128,2688]{1,0:T(8,128)(2,1)} %x_hbm.1, bf16[128,2688]{1,0:T(8,128)(2,1)} %g_hbm.1, bf16[21,256]{1,0:T(8,128)(2,1)} %wk_ref.1, bf16[21,256]{1,0:T(8,128)(2,1)} %wv_ref.1, bf16[21,512]{1,0:T(8,128)(2,1)} %wq_ref.1, bf16[21,512]{1,0:T(8,128)(2,1)} %bitcast.4, ...), custom_call_target="tpu_custom_call" | custom-call | tf_op jit(solution)/shard_map/layer_backward/pallas_call | solution.py:659
  133.3 1.3 copy.13
  134.6 1.6 %copy.14 = bf16[32,2688]{1,0:T(8,128)(2,1)} copy(bf16[32,2688]{1,0:T(8,128)(2,1)} %get-tuple-element.11) | data formatting | bytes 344064
  (2 shorter events, 0.0 us)
Async XLA Ops:
  0.6 0.7 copy-start

commit v5 on v4

--- a/solution.py
+++ b/solution.py
@@ -128,6 +128,7 @@
     HY = FZ + 15
     CY = HY + 1
     CZ = CY + 4
+    KX = CZ + 16
 
     side_z = lambda side: at_z(1 if side == 0 else -1)
     xs = (h, 1 - h)
@@ -392,9 +393,10 @@
         ctx[0, 0, :, cols] = norm_forward(acc[0:TOK, cols], k_gain, cosine, sine).astype(BF16)
     ctx[0, 1] = acc[0:TOK, 256:512].astype(BF16)
 
-    hop4 = remote(ctx.at[0], ctx.at[4], KV, shifted(4))
-    hop8 = remote(ctx.at[4], ctx.at[8], KV + 1, shifted(4))
-    hop4.start()
+    hop4 = [remote(ctx.at[0, i], ctx.at[4, i], (KV, KX)[i], shifted(4)) for i in range(2)]
+    hop8 = [remote(ctx.at[4, i], ctx.at[8, i], (KV, KX)[i] + 1, shifted(4)) for i in range(2)]
+    for copy in hop4:
+        copy.start()
 
     def side_copies(e):
         low = jnp.where(y + e < NY, 0, 4)
@@ -406,8 +408,9 @@
         @pl.when(y + e < NY)
         def _():
             side_copies(e)[0].start()
-    here(ctx.at[4], KV).wait_recv()
-    hop8.start()
+    for i in range(2):
+        here(ctx.at[4, i], (KV, KX)[i]).wait_recv()
+        hop8[i].start()
     for e in range(1, NY):
         @pl.when(y + e < NY)
         def _():
@@ -417,7 +420,8 @@
         def _():
             side_copies(e)[0].start()
     project(TOK, 3 * TOK)
-    here(ctx.at[8], KV + 1).wait_recv()
+    for i in range(2):
+        here(ctx.at[8, i], (KV, KX)[i] + 1).wait_recv()
     for e in range(1, NY):
         @pl.when(y + e >= NY)
         def _():
@@ -432,8 +436,8 @@
     for e in range(1, NY):
         here(ctx.at[e], KV + 2 * e).wait_recv()
         here(ctx.at[e + 4], KV + 2 * e + 1).wait_recv()
-    hop4.wait_send()
-    hop8.wait_send()
+    for copy in hop4 + hop8:
+        copy.wait_send()
     for e in range(1, NY):
         one, two = side_copies(e)
         one.wait_send()
@@ -538,14 +542,15 @@
     first_cols = jnp.where(iota((GROUP, FSLOT, 128), 1) < ROWS, 1.0, 0.0)
     dv_sq = (dvalue * dvalue).astype(BF16)
 
-    def slots(j, carry):
+    def slots(half, low):
+        j = 4 * half + low
         both = dot(squares[j], dv_sq)
         both = both.reshape(GROUP, FSLOT, 256)
         picked = jnp.where(first_cols > 0.5, both[:, :, 0:128], both[:, :, 128:256])
-        fpad[j // 4, pl.ds(4 * lax.rem(j, 4), 4)] = picked.astype(BF16).reshape(4, 4, FSLOT, 128)
-        return carry
-
-    lax.fori_loop(0, SEQ // GROUP, slots, 0)
+        fpad[half, 4 * low : 4 * low + 4] = picked.astype(BF16).reshape(4, 4, FSLOT, 128)
+
+    for low in range(2):
+        slots(1 - h, low)
 
     cross_low = remote(fpad.at[1 - h, pl.ds(0, 8)], flow, FH, across)
     cross_low.start()
@@ -577,8 +582,13 @@
         return first, second
 
     up_ring = ring(lambda i, yy: fpad.at[i, pl.ds(8, 8), yy], ftwo, FY)
+    for half in range(2):
+        for low in range(2, 4):
+            slots(half, low)
     for copy in up_ring:
         copy.start()
+    for low in range(2):
+        slots(h, low)
     spread_back(0, 4, 8)
     up_value = lambda i, yy: fpad[i, 8:16, yy].astype(F32)
     up_ring += ring_next(up_value, ftwo, fsend, FY)

time: 138 us -> 137 us (level)
  no operation moved by 1% of the time
where the time goes in v5:
time: 137 us; the launch traced here: 135 us
  Pallas kernels  130 us (95%)
  local copies, waits for them, and re-layouts  3.6 us (3%)
    pallas_call x1, Pallas kernels, layer(): pl.pallas_call(body, name='layer_backward', out_shape=(jax.ShapeDtypeStru...  130 us
    unnamed x4, local copies, waits for them, and re-layouts  3.6 us

profile of v5, /device:TPU:6, one launch (start us, length us, event | category | flops | bytes accessed | tf_op | source)
XLA Modules:
  0.0 135.4 jit_solution(5701093488229308807)
XLA Ops:
  0.6 0.0 copy-start
  0.6 0.6 copy-done
  1.3 1.0 multiply_sine_fusion
  2.3 130.1 %layer_backward.1 = (bf16[32,2688]{1,0:T(8,128)(2,1)}, f32[21,256]{1,0:T(8,128)}) custom-call(bf16[128,2688]{1,0:T(8,128)(2,1)} %x_hbm.1, bf16[128,2688]{1,0:T(8,128)(2,1)} %g_hbm.1, bf16[21,256]{1,0:T(8,128)(2,1)} %wk_ref.1, bf16[21,256]{1,0:T(8,128)(2,1)} %wv_ref.1, bf16[21,512]{1,0:T(8,128)(2,1)} %wq_ref.1, bf16[21,512]{1,0:T(8,128)(2,1)} %bitcast.4, ...), custom_call_target="tpu_custom_call" | custom-call | tf_op jit(solution)/shard_map/layer_backward/pallas_call | solution.py:669
  132.4 1.3 copy.13
  133.8 1.6 %copy.14 = bf16[32,2688]{1,0:T(8,128)(2,1)} copy(bf16[32,2688]{1,0:T(8,128)(2,1)} %get-tuple-element.11) | data formatting | bytes 344064
  (2 shorter events, 0.0 us)
Async XLA Ops:
  0.6 0.7 copy-start
